TPU v7x, 128 devices: a whole 4x4x4 slice. The times are simulated.
128 devices in a mesh: pair: 8 (over y_hi, x), slab: 16 (over y_lo, z, core).
Axes of the slice: x: 4, y: 4 (y_hi: 2, y_lo: 2; y = y_hi * 2 + y_lo), z: 4, core: 2. Of those that a mesh axis runs over, the one named last changes fastest.
Arguments:
- pair_density: bfloat16 [24576, 49152], P('pair', 'slab'), may hold values from -6 to 6
- subspace: bfloat16 [49152, 512], P('slab'), may hold values from -0.02734375 to 0.02734375
- band_valence: int32 [24576], P('pair'), may hold values from 0 to 510, as said below
- band_conduction: int32 [24576], P('pair'), may hold values from 1 to 511, as said below
- occupied: int32 [512], replicated, may hold values from 0 to 1, as said below
- energies: float32 [512], replicated, may hold values from -1 to 1
Outputs:
- chi_panel: float32 [512, 49152], P('pair', 'slab')
- subspace_chi: float32 [512, 512], P('slab', 'pair')
Inputs may be any that keep to these rules, and one draw needn't show every extreme that they name: Exactly half of the 512 bands are occupied. `band_valence`: every entry names a band that occupied marks as occupied. `band_conduction`: every entry names a band that occupied marks as unoccupied.
All inputs are finite; a program needn't handle non-finite values.
Results may differ from a plain program's by a relative error of at most 0.0024.
Values sent between devices are 32-bit elements; how exact they have to be, the bound alone decides.
A program may use at most 128 MiB of HBM per device.

v0:
```python
import math

import jax
import jax.numpy as jnp
from jax import lax
from jax.sharding import PartitionSpec as P


def lookup(indices, table):
    levels = jnp.arange(table.shape[0], dtype=jnp.int32)
    one_hot = (indices[:, None] == levels[None, :]).astype(jnp.float32)
    return jnp.dot(one_hot, table, precision=lax.Precision.HIGHEST)


def body(pair_density, subspace, band_valence, band_conduction, occupied, energies):
    partial_value = jnp.dot(pair_density, subspace, preferred_element_type=jnp.float32)
    coefficient = lax.psum(partial_value, "slab")
    total_pairs = pair_density.shape[0] * lax.axis_size("pair")
    band_table = jnp.stack([energies, occupied.astype(jnp.float32)], axis=1)
    valence_rows = lookup(band_valence, band_table)
    conduction_rows = lookup(band_conduction, band_table)
    scale = 1.0 / math.sqrt(total_pairs)
    pair_weight = (
        -2.0
        * valence_rows[:, 1]
        * (1.0 - conduction_rows[:, 1])
        / (jnp.abs(conduction_rows[:, 0] - valence_rows[:, 0]) + 0.5)
        * scale
    )
    weighted = (coefficient * pair_weight[:, None]).astype(jnp.bfloat16)
    chi_panel = lax.psum_scatter(
        lax.dot_general(
            weighted, pair_density, (((0,), (0,)), ((), ())), preferred_element_type=jnp.float32
        ),
        "pair",
        scatter_dimension=0,
        tiled=True,
    )
    local_sum = lax.dot_general(
        subspace.astype(jnp.float32),
        chi_panel,
        (((0,), (1,)), ((), ())),
        precision=lax.Precision.HIGHEST,
    )
    subspace_chi = lax.psum_scatter(local_sum, "slab", scatter_dimension=0, tiled=True)
    return (chi_panel, subspace_chi)


def solution(mesh):
    return jax.shard_map(
        body,
        mesh=mesh,
        in_specs=(P("pair", "slab"), P("slab", None), P("pair"), P("pair"), P(), P()),
        out_specs=(P("pair", "slab"), P("slab", "pair")),
        check_vma=False,
    )
```

profile of v0, /device:TPU:0, one launch (start us, length us, event | category | flops | bytes accessed | tf_op | source)
XLA Modules:
  0.0 350.8 jit_solution(12206670594472703781)
XLA Ops:
  7.2 0.0 copy-start
  7.2 0.0 all-reduce.2.cloned.1.call-start
  7.2 1.8 copy-done
  9.1 15.5 %fusion.12 = f32[3072,512]{1,0:T(8,128)} fusion(bf16[3072,3072]{1,0:T(8,128)(2,1)} %param.6, bf16[3072,512]{1,0:T(8,128)(2,1)S(1)} %copy-done), kind=kOutput, calls=%fused_computation.20 | convolution fusion | flops 9663676416 | bytes 28311552 | tf_op jit(solution)/shard_map/dot_general | solution.py:16
  24.5 0.0 copy-start.1
  24.5 0.0 copy-start.2
  24.5 0.0 copy-start.4
  24.5 0.0 copy-start.3
  24.6 0.0 all-reduce.2.cloned.1.call-update
  24.6 0.0 reduce-scatter.5.cloned.1.call-start
  24.6 0.6 copy-done.1
  25.2 0.0 copy-done.2
  25.3 0.0 copy-done.4
  25.3 3.3 fusion
  28.5 0.0 copy-done.3
  28.5 3.3 fusion.1
  31.8 0.1 fusion.9
  31.9 131.7 %all-reduce.2.cloned.1.call-done = f32[3072,512]{1,0:T(8,128)} async-done(((f32[3072,512]{1,0:T(8,128)}), f32[3072,512]{1,0:T(8,128)}) %all-reduce.2.cloned.1.call-update) | async-done | bytes 6291472 | tf_op jit(solution)/shard_map/psum | solution.py:17
  163.6 17.6 %fusion.2 = f32[512,3072]{1,0:T(8,128)} fusion(bf16[3072,3072]{1,0:T(8,128)(2,1)} %param.6, f32[3072,512]{1,0:T(8,128)} %all-reduce.2.cloned.1.call-done, f32[3072]{0:T(1024)S(1)} %bitcast.11), kind=kOutput, calls=%fused_computation.5 | convolution fusion | flops 9666822144 | bytes 31469568 | tf_op jit(solution)/shard_map/dot_general | solution.py:32
  181.2 0.0 reduce-scatter.5.cloned.1.call-update
  181.2 0.0 reduce-scatter.7.cloned.1.call-start
  181.3 99.2 %reduce-scatter.5.cloned.1.call-done = f32[64,3072]{1,0:T(8,128)} async-done(((f32[512,3072]{1,0:T(8,128)}), f32[64,3072]{1,0:T(8,128)}) %reduce-scatter.5.cloned.1.call-update) | async-done | bytes 786448 | tf_op jit(solution)/shard_map/reduce_scatter | solution.py:31
  280.4 2.9 convolution_bitcast_fusion
  283.3 0.8 copy.11
  284.2 0.0 reduce-scatter.7.cloned.1.call-update
  284.2 60.1 %reduce-scatter.7.cloned.1.call-done = f32[32,64]{1,0:T(8,128)} async-done(((f32[512,64]{1,0:T(8,128)}), f32[32,64]{1,0:T(8,128)}) %reduce-scatter.7.cloned.1.call-update) | async-done | bytes 8208
  (1 shorter events, 0.0 us)
Async XLA Ops:
  7.2 1.9 copy-start
  7.2 156.4 %all-reduce.2.cloned.1.call-start = ((), (), s32[]{:S(2)}) async-start(), calls=%async_computation.2 | async-start | bytes 12582912 | tf_op jit(solution)/shard_map/psum | solution.py:17
  24.5 0.7 copy-start.1
  24.5 0.7 copy-start.2
  24.5 0.7 copy-start.4
  24.5 4.0 %copy-start.3 = (s32[3072]{0:T(1024)S(1)}, s32[3072]{0:T(1024)}, u32[]{:S(2)}) copy-start(s32[3072]{0:T(1024)} %param.9) | copy-start | bytes 36868
  24.6 255.9 %reduce-scatter.5.cloned.1.call-start = ((), (), s32[]{:S(2)}) async-start(), calls=%async_computation.3 | async-start | bytes 7077888 | tf_op jit(solution)/shard_map/reduce_scatter | solution.py:31
  181.2 163.1 %reduce-scatter.7.cloned.1.call-start = ((), (), s32[]{:S(2)}) async-start(), calls=%async_computation.4 | async-start | bytes 278528
Sparse Core Ops, SparseCore 0:
  24.7 138.8 all-reduce.1
  181.3 99.0 reduce-scatter.4
  284.3 59.9 reduce-scatter.6
where the time goes:
time: 351 us
  waiting for transfers between devices  291 us (83%)
  matrix products  42.5 us (12%)
  between operations  13.8 us (4%)
    psum x1, waiting for transfers between devices, body(): coefficient = lax.psum(partial_value, 'slab')  132 us
    reduce_scatter x1, waiting for transfers between devices, body(): lax.psum_scatter(lax.dot_general(weighted, pair_density, (((0,), (0,)), (...  99.2 us
    unnamed x4, waiting for transfers between devices  60.2 us
    dot_general x1, matrix products, body(): lax.dot_general(weighted, pair_density, (((0,), (0,)), ((), ())), preferr...  17.6 us
    dot_general x1, matrix products, body(): jnp.dot(pair_density, subspace, preferred_element_type=jnp.float32)  15.5 us
  transfers between devices with their start and end apart: 3, of which 3 were waited for; matrix products, arithmetic and copies ran while one was open for 2% of the time, Pallas kernels for 0%

commit v1 on v0

v1 whole, which is shorter than its diff:
```python
import functools
import math

import jax
import jax.numpy as jnp
from jax import lax
from jax.experimental import pallas as pl
from jax.experimental.pallas import tpu as pltpu
from jax.sharding import PartitionSpec as P

MESH = pl.DeviceIdType.MESH
F32, BF16 = jnp.float32, jnp.bfloat16

CHUNKS = 4
PARTS = 2
SUM_MODE = "BBBB"
PANEL_MODE = "BBBB"
ORDER = (
    ("A",), ("B", 0), ("B", 1), ("R1", 0), ("R1", 1), ("B", 2), ("B", 3), ("R2", 0),
    ("R1", 2), ("R1", 3), ("R2", 1), ("R3", 0), ("R2", 2), ("R2", 3), ("R3", 1), ("R4", 0),
    ("R3", 2), ("R3", 3), ("R4", 1), ("G2", 0), ("R4", 2), ("R4", 3), ("G2", 1), ("G3", 0),
    ("G4", 0), ("G2", 2), ("W", 0), ("G2", 3), ("F1", 0, 0), ("G3", 1), ("F1", 0, 1), ("G3", 2),
    ("G4", 1), ("G3", 3), ("F2", 0, 0), ("W", 1), ("G4", 2), ("F2", 0, 1), ("F1", 1, 0), ("G4", 3),
    ("F3", 0, 0), ("F3", 0, 1), ("F1", 1, 1), ("W", 2), ("F1", 2, 0), ("F4", 0, 0), ("F2", 1, 0), ("F1", 2, 1),
    ("F4", 0, 1), ("W", 3), ("F2", 1, 1), ("F1", 3, 0), ("F3", 1, 0), ("F2", 2, 0), ("F1", 3, 1), ("F2", 2, 1),
    ("F3", 1, 1), ("S1",), ("F2", 3, 0), ("F4", 1, 0), ("F3", 2, 0), ("F2", 3, 1), ("F3", 2, 1), ("F4", 1, 1),
    ("S2",), ("F3", 3, 0), ("F4", 2, 0), ("F3", 3, 1), ("F4", 2, 1), ("F4", 3, 0), ("F4", 3, 1),
)


def lookup(indices, table):
    levels = jnp.arange(table.shape[0], dtype=jnp.int32)
    one_hot = (indices[:, None] == levels[None, :]).astype(F32)
    return jnp.dot(one_hot, table, precision=lax.Precision.HIGHEST)


class Links:
    def __init__(self, send_sem, recv_sem):
        self.send_sem, self.recv_sem = send_sem, recv_sem
        self.made = {}

    def send(self, name, source, target, device):
        at = len(self.made)
        copy = pltpu.make_async_remote_copy(
            source, target, self.send_sem.at[at], self.recv_sem.at[at], device_id=device, device_id_type=MESH
        )
        copy.start()
        self.made[name] = copy

    def wait(self, *names):
        for name in names:
            self.made[name].wait_recv()

    def finish(self):
        for copy in self.made.values():
            copy.wait_send()


def ring_sum(links, tag, mode, piece, slots, ring_up, ring_down, across, half):
    lo, hi = pl.ds(0, half), pl.ds(half, half)

    def add(ref, *others):
        total = ref[...]
        for other in others:
            total = total + other[...]
        ref[...] = total

    def first():
        if mode == "B":
            links.send((tag, "y1"), piece(2, 1), slots.at[6], across)
            links.send((tag, "p1"), piece(1, 1), slots.at[0], ring_up)
            links.send((tag, "m1"), piece(3, 1), slots.at[1], ring_down)
        else:
            links.send((tag, "p2"), piece(2, 0), slots.at[2], ring_up)
            links.send((tag, "m2"), piece(2, 1), slots.at[3], ring_down)
            links.send((tag, "p1"), piece(1, 1), slots.at[0], ring_up)
            links.send((tag, "m1"), piece(3, 0), slots.at[1], ring_down)

    def second():
        if mode == "B":
            links.wait((tag, "y1"))
            add(piece(2, 0), slots.at[6])
            links.send((tag, "p2"), piece(2, 0).at[lo], slots.at[2, lo], ring_up)
            links.send((tag, "m2"), piece(2, 0).at[hi], slots.at[3, hi], ring_down)
        else:
            links.wait((tag, "p2"))
            add(piece(1, 0), slots.at[2])
            links.send((tag, "p3"), piece(1, 0), slots.at[4], ring_up)
            links.wait((tag, "m2"))
            add(piece(3, 1), slots.at[3])
            links.send((tag, "m3"), piece(3, 1), slots.at[5], ring_down)

    def third():
        if mode == "B":
            links.wait((tag, "p1"), (tag, "m1"))
            add(piece(0, 1), slots.at[0], slots.at[1])
            links.send((tag, "y3"), piece(0, 1), slots.at[7], across)
            links.wait((tag, "p2"))
            add(piece(1, 0).at[lo], slots.at[2, lo])
            links.send((tag, "p3"), piece(1, 0), slots.at[4], ring_up)
            links.wait((tag, "m2"))
            add(piece(3, 0).at[hi], slots.at[3, hi])
            links.send((tag, "m3"), piece(3, 0), slots.at[5], ring_down)
        else:
            links.wait((tag, "p1"), (tag, "m3"))
            add(piece(0, 1), slots.at[0], slots.at[5])
            links.send((tag, "y3"), piece(0, 1), slots.at[7], across)

    def last():
        if mode == "B":
            links.wait((tag, "y3"), (tag, "p3"), (tag, "m3"))
            return piece(0, 0)[...] + slots[4] + slots[5] + slots[7]
        links.wait((tag, "m1"), (tag, "p3"), (tag, "y3"))
        return piece(0, 0)[...] + slots[1] + slots[4] + slots[7]

    return first, second, third, last


def kernel(
    a_hbm, s_hbm, w_ref, chi_out, sub_out,
    a_v, s_v, sp, coeff, core_in, sum_in, full, wt, chi, panel_in, sub_mine, sub_in,
    load_sem, core_send, core_recv, send_sem, recv_sem,
):
    pairs, depth = a_v.shape
    nb = s_v.shape[1]
    width = nb // CHUNKS
    block = pairs // 8
    own = block // 2
    rows_q = width // 8
    cols = depth // PARTS

    pair, slab = lax.axis_index("pair"), lax.axis_index("slab")
    y_hi, x = lax.div(pair, 4), lax.rem(pair, 4)
    y_lo, z, core = lax.div(slab, 8), lax.rem(lax.div(slab, 2), 4), lax.rem(slab, 2)

    def slab_of(y, zz, c):
        return (pair, y * 8 + zz * 2 + c)

    def pair_of(y, xx):
        return (y * 4 + xx, slab)

    def up(v, d):
        return lax.rem(v + d, 4)

    z_up, z_down = slab_of(y_lo, up(z, 1), core), slab_of(y_lo, up(z, 3), core)
    y_across, other_core = slab_of(1 - y_lo, z, core), slab_of(y_lo, z, 1 - core)
    x_up, x_down, hi_across = pair_of(y_hi, up(x, 1)), pair_of(y_hi, up(x, 3)), pair_of(1 - y_hi, x)

    def peer(d):
        return (lax.rem(pair + d, 8), slab)

    Z_ORDER = (2, 1, 3, 0)

    def nth_z(j):
        step = jnp.where(j == 0, 2, jnp.where(j == 1, 1, jnp.where(j == 2, 3, 0)))
        return lax.rem(z + step, 4)

    def nth_rows(i):
        other = jnp.where(i < 4, 1 - core, core)
        j = lax.rem(i, 4)
        return pl.ds(pl.multiple_of((other * 4 + nth_z(j)) * block, block), block)

    def a_load(i):
        return pltpu.make_async_copy(a_hbm.at[nth_rows(i)], a_v.at[nth_rows(i)], load_sem.at[i])

    s_load = pltpu.make_async_copy(s_hbm, s_v, load_sem.at[8])
    s_load.start()
    for i in range(8):
        a_load(i).start()

    barrier = pltpu.get_barrier_semaphore()
    greeted = [z_up, z_down, y_across, other_core] + [peer(d) for d in range(1, 8)]
    for device in greeted:
        pl.semaphore_signal(barrier, inc=1, device_id=device, device_id_type=MESH)

    links = Links(send_sem, recv_sem)

    def choose(kp):
        to = lax.broadcasted_iota(jnp.int32, (nb, 2 * width), 1)
        frm = lax.broadcasted_iota(jnp.int32, (nb, 2 * width), 0)
        k = kp * 2 + to // width
        b = (lax.rem(to, width) // rows_q) * (nb // 8) + k * rows_q + lax.rem(to, rows_q)
        pick = jnp.where(frm == b, 1.0, 0.0).astype(BF16)

        @pl.loop(0, 8)
        def _(i):
            rows = pl.ds(pl.multiple_of(i * block, block), block)
            sp[rows, :] = jnp.dot(s_v[rows, :], pick, preferred_element_type=F32).astype(BF16)

    def core_copy(k, j):
        there = pl.ds(pl.multiple_of(nth_z(j) * block, block), block)
        return pltpu.make_async_remote_copy(
            coeff.at[k, nth_rows(j)], core_in.at[k, there], core_send.at[k, j], core_recv.at[k, j],
            device_id=other_core, device_id_type=MESH,
        )

    def product(kp, start, stop):
        @pl.loop(start, stop)
        def _(i):
            rows = nth_rows(i)
            if kp == 0:
                a_load(i).wait()
            part = jnp.dot(a_v[rows, :], sp[...], preferred_element_type=F32)
            for h in range(2):
                coeff[2 * kp + h, rows, :] = part[:, h * width : (h + 1) * width]

            @pl.when(i < 4)
            def _():
                for h in range(2):
                    core_copy(2 * kp + h, i).start()

    def owner_rows(z_at, y_at):
        return pl.ds(pl.multiple_of((core * 4 + z_at) * block + y_at * own, own), own)

    steps = {}
    for k in range(CHUNKS):
        get = lambda dr, da, k=k: coeff.at[k, owner_rows(up(z, dr), (1 - y_lo) if da else y_lo)]
        first, second, third, last = ring_sum(
            links, ("R", k), SUM_MODE[k], get, sum_in.at[k], z_up, z_down, y_across, own // 2
        )

        def r1(k=k, first=first):
            for j in range(4):
                core_copy(k, j).wait_recv()
                here = pl.ds(pl.multiple_of((core * 4 + nth_z(j)) * block, block), block)
                there = pl.ds(pl.multiple_of(nth_z(j) * block, block), block)
                coeff[k, here, :] = coeff[k, here, :] + core_in[k, there, :]
            first()

        def spread(name, z_at, y_at, device, k=k, part=None):
            rows = owner_rows(z_at, y_at)
            if part is not None:
                start = (core * 4 + z_at) * block + y_at * own + part * (own // 2)
                rows = pl.ds(pl.multiple_of(start, own // 2), own // 2)
            links.send((name, k), full.at[k, rows], full.at[k, rows], device)

        def r4(k=k, last=last, spread=spread):
            full[k, owner_rows(z, y_lo), :] = last()
            spread("y1", z, y_lo, y_across)
            spread("p1", z, y_lo, z_up)
            spread("m1", z, y_lo, z_down)
            spread("c0", z, y_lo, other_core)

        def g2(k=k, spread=spread):
            links.wait(("p1", k))
            spread("p2", up(z, 3), y_lo, z_up, part=0)
            links.wait(("m1", k))
            spread("m2", up(z, 1), y_lo, z_down, part=1)
            links.wait(("y1", k))
            spread("p3", z, 1 - y_lo, z_up)
            spread("m3", z, 1 - y_lo, z_down)
            spread("c1", up(z, 3), y_lo, other_core)
            spread("c2", up(z, 1), y_lo, other_core)
            spread("c3", z, 1 - y_lo, other_core)

        def g3(k=k, spread=spread):
            links.wait(("p2", k), ("m2", k))
            spread("y3", up(z, 2), y_lo, y_across)
            spread("c4", up(z, 2), y_lo, other_core)

        def g4(k=k, spread=spread):
            links.wait(("p3", k), ("m3", k))
            spread("c5", up(z, 3), 1 - y_lo, other_core)
            spread("c6", up(z, 1), 1 - y_lo, other_core)
            links.wait(("y3", k))
            spread("c7", up(z, 2), 1 - y_lo, other_core)

        def weigh(k=k):
            links.wait(*[(f"c{i}", k) for i in range(8)])

            @pl.loop(0, 8)
            def _(i):
                at = pl.ds(pl.multiple_of(i * block, block), block)
                wt[k, :, at] = (full[k, at, :].T * w_ref[:, at]).astype(BF16)

        steps["R1", k], steps["R2", k], steps["R3", k], steps["R4", k] = r1, second, third, r4
        steps["G2", k], steps["G3", k], steps["G4", k], steps["W", k] = g2, g3, g4, weigh

        for g in range(PARTS):
            def rows_of(dx, dy, k=k, g=g):
                q = ((1 - y_hi) if dy else y_hi) * 4 + up(x, dx)
                return chi.at[k, g, pl.ds(pl.multiple_of(q * rows_q, rows_q), rows_q)]

            first, second, third, last = ring_sum(
                links, ("F", k, g), PANEL_MODE[k], rows_of, panel_in.at[k, g], x_up, x_down, hi_across, rows_q // 2
            )

            def f1(k=k, g=g, first=first):
                tile = cols // 3

                @pl.loop(0, 3)
                def _(i):
                    src = pl.ds(pl.multiple_of(g * cols + i * tile, tile), tile)
                    dst = pl.ds(pl.multiple_of(i * tile, tile), tile)
                    chi[k, g, :, dst] = jnp.dot(wt[k], a_v[:, src], preferred_element_type=F32)

                first()

            def f4(k=k, g=g, last=last):
                chi_out[k * rows_q : (k + 1) * rows_q, g * cols : (g + 1) * cols] = last()

            steps["F1", k, g], steps["F2", k, g], steps["F3", k, g], steps["F4", k, g] = f1, second, third, f4

    steps["A",] = lambda: product(0, 0, 8)

    def b0():
        choose(1)
        product(1, 0, 2)

    steps["B", 0] = b0
    for i in range(1, 4):
        steps["B", i] = functools.partial(product, 1, 2 * i, 2 * i + 2)

    def s1():
        @pl.loop(0, 8)
        def _(i):
            at = pl.ds(pl.multiple_of(i * block, block), block)
            for h in range(2):
                value = full[2 * core + h, at, :]
                high = value.astype(BF16)
                s_v[at, 2 * h * width : (2 * h + 1) * width] = high
                s_v[at, (2 * h + 1) * width : (2 * h + 2) * width] = (value - high.astype(F32)).astype(BF16)

        q = lax.div(slab, 2)
        lane = lax.broadcasted_iota(jnp.int32, (width, width), 1)
        for k in range(CHUNKS):
            part = jnp.dot(wt[k], s_v[...], preferred_element_type=F32)
            even = part[:, :width] + part[:, width : 2 * width]
            odd = part[:, 2 * width : 3 * width] + part[:, 3 * width :]
            even = pltpu.roll(even, lax.rem(width - q * rows_q, width), 1)
            odd = pltpu.roll(odd, lax.rem(width + rows_q - q * rows_q, width), 1)
            mine = jnp.where(lane < rows_q, even, jnp.where(lane < 2 * rows_q, odd, 0.0))
            for o in range(8):
                sub_mine[o, k * rows_q : (k + 1) * rows_q, :] = mine[o * rows_q : (o + 1) * rows_q]
        for d in range(1, 8):
            links.send(("s", d), sub_mine.at[lax.rem(pair + d, 8)], sub_in.at[d - 1], peer(d))

    def s2():
        total = sub_mine[pair]
        for d in range(1, 8):
            links.wait(("s", d))
            total = total + sub_in[d - 1]
        square = jnp.concatenate([total, jnp.zeros_like(total)], axis=0)
        sub_out[...] = square.T[: 2 * rows_q, : 4 * rows_q]

    steps["S1",], steps["S2",] = s1, s2

    s_load.wait()
    choose(0)
    pl.semaphore_wait(barrier, len(greeted))
    assert sorted(ORDER, key=str) == sorted(steps, key=str)
    for name in ORDER:
        steps[name]()
    links.finish()
    for k in range(CHUNKS):
        for j in range(4):
            core_copy(k, j).wait_send()


def body(pair_density, subspace, band_valence, band_conduction, occupied, energies):
    pairs, depth = pair_density.shape
    nb = subspace.shape[1]
    total_pairs = pairs * lax.axis_size("pair")
    band_table = jnp.stack([energies, occupied.astype(F32)], axis=1)
    valence_rows = lookup(band_valence, band_table)
    conduction_rows = lookup(band_conduction, band_table)
    scale = 1.0 / math.sqrt(total_pairs)
    pair_weight = (
        -2.0
        * valence_rows[:, 1]
        * (1.0 - conduction_rows[:, 1])
        / (jnp.abs(conduction_rows[:, 0] - valence_rows[:, 0]) + 0.5)
        * scale
    )
    width, own, rows_q, cols = nb // CHUNKS, pairs // 16, nb // CHUNKS // 8, depth // PARTS
    copies = CHUNKS * (8 + 8 + 8) + CHUNKS * PARTS * 8 + 7
    vmem, dma = pltpu.VMEM, pltpu.SemaphoreType.DMA
    return pl.pallas_call(
        kernel,
        name="project",
        out_shape=(
            jax.ShapeDtypeStruct((nb // 8, depth), F32),
            jax.ShapeDtypeStruct((nb // 16, nb // 8), F32),
        ),
        in_specs=[
            pl.BlockSpec(memory_space=pl.ANY),
            pl.BlockSpec(memory_space=pl.ANY),
            pl.BlockSpec(memory_space=vmem),
        ],
        out_specs=(pl.BlockSpec(memory_space=vmem), pl.BlockSpec(memory_space=vmem)),
        scratch_shapes=[
            vmem((pairs, depth), BF16),
            vmem((depth, nb), BF16),
            vmem((depth, 2 * width), BF16),
            vmem((CHUNKS, pairs, width), F32),
            vmem((CHUNKS, pairs // 2, width), F32),
            vmem((CHUNKS, 8, own, width), F32),
            vmem((CHUNKS, pairs, width), F32),
            vmem((CHUNKS, width, pairs), BF16),
            vmem((CHUNKS, PARTS, width, cols), F32),
            vmem((CHUNKS, PARTS, 8, rows_q, cols), F32),
            vmem((8, nb // 8, width), F32),
            vmem((7, nb // 8, width), F32),
            dma((9,)),
            dma((CHUNKS, 4)),
            dma((CHUNKS, 4)),
            dma((copies,)),
            dma((copies,)),
        ],
        compiler_params=pltpu.CompilerParams(
            collective_id=0, has_side_effects=True, vmem_limit_bytes=67043328
        ),
    )(pair_density, subspace, pair_weight[None, :])


def solution(mesh):
    return jax.shard_map(
        body,
        mesh=mesh,
        in_specs=(P("pair", "slab"), P("slab", None), P("pair"), P("pair"), P(), P()),
        out_specs=(P("pair", "slab"), P("slab", "pair")),
        check_vma=False,
    )
```

time: 351 us -> 130 us (0.37)
  waiting for transfers between devices: 291 us -> 0 us
  Pallas kernels: 0 us -> 116 us
  matrix products: 42.5 us -> 7.91 us
  between operations: 13.8 us -> 0.64 us
    psum x1 -> x0, waiting for transfers between devices: 132 us -> none  [body(): coefficient = lax.psum(partial_value, 'slab')]
    pallas_call x0 -> x1, Pallas kernels: none -> 116 us  [body(): pl.pallas_call(kernel, name='project', out_shape=(jax.ShapeDtypeStruct((n...]
    reduce_scatter x1 -> x0, waiting for transfers between devices: 99.2 us -> none  [body(): lax.psum_scatter(lax.dot_general(weighted, pair_density, (((0,), (0,)), (...]
    unnamed x4 -> x0, waiting for transfers between devices: 60.2 us -> none
    dot_general x3 -> x0, matrix products: 35.9 us -> none  [the longest x1 17.6 us: body(): lax.dot_general(weighted, pair_density, (((0,), (0,)), ((), ())), preferr...]
  transfers between devices with their start and end apart: 3 -> 0, of which waited for: 3 -> 0; matrix products, arithmetic and copies ran while one was open for 2% -> 0% of each run, Pallas kernels for 0% -> 0%
where the time goes in v1:
time: 130 us
  Pallas kernels  116 us (89%)
  matrix products  7.91 us (6%)
  local copies, waits for them, and re-layouts  3.39 us (3%)
  other arithmetic  1.35 us (1%)
    pallas_call x1, Pallas kernels, body(): pl.pallas_call(kernel, name='project', out_shape=(jax.ShapeDtypeStruct((n...  116 us
    dot_general x2, matrix products, lookup(): return jnp.dot(one_hot, table, precision=lax.Precision.HIGHEST)  7.91 us
    unnamed x2, local copies, waits for them, and re-layouts  3.39 us

profile of v1, /device:TPU:0, one launch (start us, length us, event | category | flops | bytes accessed | tf_op | source)
XLA Modules:
  0.0 129.6 jit_solution(7427481233640305505)
XLA Ops:
  0.6 0.7 convert_element_type.2
  1.3 4.0 %fusion.1 = f32[3072,2]{0,1:T(2,128)S(1)} fusion(s32[3072]{0:T(1024)} %param.9, f32[512,1]{0,1:T(1,128)S(1)} %bitcast.4, f32[512,1]{0,1:T(1,128)} %bitcast.6), kind=kOutput, calls=%fused_computation.3 | convolution fusion | flops 39322624 | bytes 40960 | tf_op jit(solution)/shard_map/dot_general | solution.py:34
  5.3 4.0 %fusion = f32[3072,2]{0,1:T(2,128)S(1)} fusion(s32[3072]{0:T(1024)} %param.8, f32[512,1]{0,1:T(1,128)S(1)} %bitcast.5, f32[512,1]{0,1:T(1,128)} %bitcast.7), kind=kOutput, calls=%fused_computation.2 | convolution fusion | flops 39322624 | bytes 40960 | tf_op jit(solution)/shard_map/dot_general | solution.py:34
  9.2 0.7 multiply_bitcast_fusion.w_ref
  9.9 116.4 %project.1 = (f32[64,3072]{1,0:T(8,128)}, f32[32,64]{1,0:T(8,128)}) custom-call(bf16[3072,3072]{1,0:T(8,128)(2,1)} %a_hbm.1, bf16[3072,512]{1,0:T(8,128)(2,1)} %s_hbm.1, f32[1,3072]{1,0:T(1,128)} %multiply_bitcast_fusion.w_ref), custom_call_target="tpu_custom_call" | custom-call | tf_op jit(solution)/shard_map/project/pallas_call | solution.py:378
  126.3 2.1 %copy.10 = f32[64,3072]{1,0:T(8,128)} copy(f32[64,3072]{1,0:T(8,128)} %get-tuple-element.4) | data formatting | bytes 1572864
  128.3 1.3 %copy.11 = f32[32,64]{1,0:T(8,128)} copy(f32[32,64]{1,0:T(8,128)} %get-tuple-element.5) | data formatting | bytes 16384

commit v2 on v1

--- a/solution.py
+++ b/solution.py
@@ -14,24 +14,24 @@
 CHUNKS = 4
 PARTS = 2
 SUM_MODE = "BBBB"
+SPREAD_MODE = "BABA"
 PANEL_MODE = "BBBB"
 ORDER = (
-    ("A",), ("B", 0), ("B", 1), ("R1", 0), ("R1", 1), ("B", 2), ("B", 3), ("R2", 0),
-    ("R1", 2), ("R1", 3), ("R2", 1), ("R3", 0), ("R2", 2), ("R2", 3), ("R3", 1), ("R4", 0),
-    ("R3", 2), ("R3", 3), ("R4", 1), ("G2", 0), ("R4", 2), ("R4", 3), ("G2", 1), ("G3", 0),
-    ("G4", 0), ("G2", 2), ("W", 0), ("G2", 3), ("F1", 0, 0), ("G3", 1), ("F1", 0, 1), ("G3", 2),
-    ("G4", 1), ("G3", 3), ("F2", 0, 0), ("W", 1), ("G4", 2), ("F2", 0, 1), ("F1", 1, 0), ("G4", 3),
-    ("F3", 0, 0), ("F3", 0, 1), ("F1", 1, 1), ("W", 2), ("F1", 2, 0), ("F4", 0, 0), ("F2", 1, 0), ("F1", 2, 1),
-    ("F4", 0, 1), ("W", 3), ("F2", 1, 1), ("F1", 3, 0), ("F3", 1, 0), ("F2", 2, 0), ("F1", 3, 1), ("F2", 2, 1),
-    ("F3", 1, 1), ("S1",), ("F2", 3, 0), ("F4", 1, 0), ("F3", 2, 0), ("F2", 3, 1), ("F3", 2, 1), ("F4", 1, 1),
-    ("S2",), ("F3", 3, 0), ("F4", 2, 0), ("F3", 3, 1), ("F4", 2, 1), ("F4", 3, 0), ("F4", 3, 1),
+    ("A", 0), ("A", 1), ("A", 2), ("Q", 0, 0), ("Q", 0, 1), ("A", 3), ("Q", 0, 2), ("Q", 1, 0),
+    ("Q", 1, 1), ("Q", 0, 3), ("R2", 0), ("Q", 1, 2), ("Q", 1, 3), ("B", 0), ("R3", 0), ("R2", 1),
+    ("R5", 0), ("B", 1), ("R3", 1), ("R5", 1), ("B", 2), ("R4", 0), ("Q", 2, 0), ("R4", 1),
+    ("B", 3), ("G2", 0), ("Q", 2, 1), ("G5", 0), ("L", 2), ("Q", 2, 2), ("G3", 0), ("G5", 1),
+    ("Q", 2, 3), ("Q", 3, 0), ("L", 0), ("R2", 2), ("L", 1), ("Q", 3, 1), ("G4", 0), ("G2", 1),
+    ("L", 3), ("Q", 3, 2), ("W", 0), ("R3", 2), ("G3", 1), ("Q", 3, 3), ("R2", 3), ("F1", 0, 0),
+    ("R3", 3), ("R5", 2), ("F1", 0, 1), ("G4", 1), ("R5", 3), ("F2", 0, 0), ("R4", 2), ("W", 1),
+    ("F1", 1, 0), ("G2", 2), ("G5", 2), ("F5", 0, 0), ("F2", 0, 1), ("R4", 3), ("G3", 2), ("F1", 1, 1),
+    ("F2", 1, 0), ("G5", 3), ("G4", 2), ("G2", 3), ("F5", 0, 1), ("F3", 0, 0), ("G3", 3), ("W", 2),
+    ("F5", 1, 0), ("F2", 1, 1), ("F3", 1, 0), ("F1", 2, 0), ("G4", 3), ("F1", 2, 1), ("F5", 1, 1), ("W", 3),
+    ("F2", 2, 0), ("F3", 0, 1), ("F1", 3, 0), ("F3", 1, 1), ("F1", 3, 1), ("F2", 2, 1), ("F2", 3, 0), ("F4", 1, 0),
+    ("F3", 2, 0), ("F5", 2, 0), ("S1",), ("F3", 3, 0), ("F4", 1, 1), ("F4", 0, 0), ("F2", 3, 1), ("F5", 2, 1),
+    ("F3", 3, 1), ("F3", 2, 1), ("F5", 3, 1), ("F4", 0, 1), ("S2",), ("F5", 3, 0), ("F4", 3, 1), ("F4", 2, 1),
+    ("F4", 2, 0), ("F4", 3, 0),
 )
-
-
-def lookup(indices, table):
-    levels = jnp.arange(table.shape[0], dtype=jnp.int32)
-    one_hot = (indices[:, None] == levels[None, :]).astype(F32)
-    return jnp.dot(one_hot, table, precision=lax.Precision.HIGHEST)
 
 
 class Links:
@@ -65,16 +65,22 @@
             total = total + other[...]
         ref[...] = total
 
-    def first():
+    def first(j):
         if mode == "B":
-            links.send((tag, "y1"), piece(2, 1), slots.at[6], across)
-            links.send((tag, "p1"), piece(1, 1), slots.at[0], ring_up)
-            links.send((tag, "m1"), piece(3, 1), slots.at[1], ring_down)
+            if j == 0:
+                links.send((tag, "y1"), piece(2, 1), slots.at[6], across)
+            if j == 1:
+                links.send((tag, "p1"), piece(1, 1), slots.at[0], ring_up)
+            if j == 2:
+                links.send((tag, "m1"), piece(3, 1), slots.at[1], ring_down)
         else:
-            links.send((tag, "p2"), piece(2, 0), slots.at[2], ring_up)
-            links.send((tag, "m2"), piece(2, 1), slots.at[3], ring_down)
-            links.send((tag, "p1"), piece(1, 1), slots.at[0], ring_up)
-            links.send((tag, "m1"), piece(3, 0), slots.at[1], ring_down)
+            if j == 0:
+                links.send((tag, "p2"), piece(2, 0), slots.at[2], ring_up)
+                links.send((tag, "m2"), piece(2, 1), slots.at[3], ring_down)
+            if j == 1:
+                links.send((tag, "p1"), piece(1, 1), slots.at[0], ring_up)
+            if j == 2:
+                links.send((tag, "m1"), piece(3, 0), slots.at[1], ring_down)
 
     def second():
         if mode == "B":
@@ -95,16 +101,18 @@
             links.wait((tag, "p1"), (tag, "m1"))
             add(piece(0, 1), slots.at[0], slots.at[1])
             links.send((tag, "y3"), piece(0, 1), slots.at[7], across)
-            links.wait((tag, "p2"))
-            add(piece(1, 0).at[lo], slots.at[2, lo])
-            links.send((tag, "p3"), piece(1, 0), slots.at[4], ring_up)
-            links.wait((tag, "m2"))
-            add(piece(3, 0).at[hi], slots.at[3, hi])
-            links.send((tag, "m3"), piece(3, 0), slots.at[5], ring_down)
         else:
             links.wait((tag, "p1"), (tag, "m3"))
             add(piece(0, 1), slots.at[0], slots.at[5])
             links.send((tag, "y3"), piece(0, 1), slots.at[7], across)
+
+    def fourth():
+        links.wait((tag, "p2"))
+        add(piece(1, 0).at[lo], slots.at[2, lo])
+        links.send((tag, "p3"), piece(1, 0), slots.at[4], ring_up)
+        links.wait((tag, "m2"))
+        add(piece(3, 0).at[hi], slots.at[3, hi])
+        links.send((tag, "m3"), piece(3, 0), slots.at[5], ring_down)
 
     def last():
         if mode == "B":
@@ -113,12 +121,12 @@
         links.wait((tag, "m1"), (tag, "p3"), (tag, "y3"))
         return piece(0, 0)[...] + slots[1] + slots[4] + slots[7]
 
-    return first, second, third, last
+    return first, second, third, fourth, last
 
 
 def kernel(
-    a_hbm, s_hbm, w_ref, chi_out, sub_out,
-    a_v, s_v, sp, coeff, core_in, sum_in, full, wt, chi, panel_in, sub_mine, sub_in,
+    a_hbm, s_hbm, valence_ref, conduction_ref, occupied_ref, energies_ref, chi_out, sub_out,
+    w_ref, a_v, s_v, sp, coeff, core_in, sum_in, full, wt, chi, panel_in, sub_mine, sub_in,
     load_sem, core_send, core_recv, send_sem, recv_sem,
 ):
     pairs, depth = a_v.shape
@@ -151,22 +159,24 @@
 
     Z_ORDER = (2, 1, 3, 0)
 
-    def nth_z(j):
-        step = jnp.where(j == 0, 2, jnp.where(j == 1, 1, jnp.where(j == 2, 3, 0)))
-        return lax.rem(z + step, 4)
-
-    def nth_rows(i):
-        other = jnp.where(i < 4, 1 - core, core)
-        j = lax.rem(i, 4)
-        return pl.ds(pl.multiple_of((other * 4 + nth_z(j)) * block, block), block)
-
-    def a_load(i):
-        return pltpu.make_async_copy(a_hbm.at[nth_rows(i)], a_v.at[nth_rows(i)], load_sem.at[i])
+    def block_rows(core_at, j):
+        return pl.ds(pl.multiple_of((core_at * 4 + up(z, Z_ORDER[j])) * block, block), block)
+
+    def half_rows(j):
+        return pl.ds(pl.multiple_of(up(z, Z_ORDER[j]) * block, block), block)
+
+    def side(i):
+        return jnp.where(i == 0, 1 - core, core)
+
+    def a_load(j, i):
+        rows = block_rows(side(i), j)
+        return pltpu.make_async_copy(a_hbm.at[rows], a_v.at[rows], load_sem.at[2 * j + i])
 
     s_load = pltpu.make_async_copy(s_hbm, s_v, load_sem.at[8])
     s_load.start()
-    for i in range(8):
-        a_load(i).start()
+    for j in range(4):
+        for i in range(2):
+            a_load(j, i).start()
 
     barrier = pltpu.get_barrier_semaphore()
     greeted = [z_up, z_down, y_across, other_core] + [peer(d) for d in range(1, 8)]
@@ -188,26 +198,47 @@
             sp[rows, :] = jnp.dot(s_v[rows, :], pick, preferred_element_type=F32).astype(BF16)
 
     def core_copy(k, j):
-        there = pl.ds(pl.multiple_of(nth_z(j) * block, block), block)
         return pltpu.make_async_remote_copy(
-            coeff.at[k, nth_rows(j)], core_in.at[k, there], core_send.at[k, j], core_recv.at[k, j],
+            coeff.at[k, block_rows(1 - core, j)], core_in.at[k, half_rows(j)], core_send.at[k, j], core_recv.at[k, j],
             device_id=other_core, device_id_type=MESH,
         )
 
-    def product(kp, start, stop):
-        @pl.loop(start, stop)
+    def product(kp, j):
+        @pl.loop(0, 2)
         def _(i):
-            rows = nth_rows(i)
+            rows = block_rows(side(i), j)
             if kp == 0:
-                a_load(i).wait()
+                a_load(j, i).wait()
             part = jnp.dot(a_v[rows, :], sp[...], preferred_element_type=F32)
             for h in range(2):
                 coeff[2 * kp + h, rows, :] = part[:, h * width : (h + 1) * width]
 
-            @pl.when(i < 4)
+            @pl.when(i == 0)
             def _():
                 for h in range(2):
-                    core_copy(2 * kp + h, i).start()
+                    core_copy(2 * kp + h, j).start()
+
+    def weights(j):
+        at = slice(j * (pairs // 4), (j + 1) * (pairs // 4))
+        bands = energies_ref.shape[1]
+        energy = energies_ref[...]
+        high = energy.astype(BF16).astype(F32)
+        middle = (energy - high).astype(BF16).astype(F32)
+        low = energy - high - middle
+        row = lax.broadcasted_iota(jnp.int32, (16, bands), 0)
+        table = jnp.where(row == 0, high, jnp.where(row == 1, middle, jnp.where(row == 2, low, 0.0)))
+        table = jnp.where(row == 3, occupied_ref[...].astype(F32), table).astype(BF16)
+        band = lax.broadcasted_iota(jnp.int32, (bands, pairs // 4), 0)
+
+        def lookup(indices):
+            one_hot = jnp.where(band == indices, 1.0, 0.0).astype(BF16)
+            found = jnp.dot(table, one_hot, preferred_element_type=F32)
+            return found[0:1] + found[1:2] + found[2:3], found[3:4]
+
+        energy_low, filled_low = lookup(valence_ref[:, at])
+        energy_high, filled_high = lookup(conduction_ref[:, at])
+        scale = 1.0 / math.sqrt(pairs * 8)
+        w_ref[:, at] = -2.0 * filled_low * (1.0 - filled_high) / (jnp.abs(energy_high - energy_low) + 0.5) * scale
 
     def owner_rows(z_at, y_at):
         return pl.ds(pl.multiple_of((core * 4 + z_at) * block + y_at * own, own), own)
@@ -215,17 +246,18 @@
     steps = {}
     for k in range(CHUNKS):
         get = lambda dr, da, k=k: coeff.at[k, owner_rows(up(z, dr), (1 - y_lo) if da else y_lo)]
-        first, second, third, last = ring_sum(
+        first, second, third, fourth, last = ring_sum(
             links, ("R", k), SUM_MODE[k], get, sum_in.at[k], z_up, z_down, y_across, own // 2
         )
 
-        def r1(k=k, first=first):
-            for j in range(4):
-                core_copy(k, j).wait_recv()
-                here = pl.ds(pl.multiple_of((core * 4 + nth_z(j)) * block, block), block)
-                there = pl.ds(pl.multiple_of(nth_z(j) * block, block), block)
-                coeff[k, here, :] = coeff[k, here, :] + core_in[k, there, :]
-            first()
+        def gather(j, k=k, first=first):
+            core_copy(k, j).wait_recv()
+            here = block_rows(core, j)
+            coeff[k, here, :] = coeff[k, here, :] + core_in[k, half_rows(j), :]
+            first(j)
+
+        for j in range(4):
+            steps["Q", k, j] = functools.partial(gather, j)
 
         def spread(name, z_at, y_at, device, k=k, part=None):
             rows = owner_rows(z_at, y_at)
@@ -241,28 +273,44 @@
             spread("m1", z, y_lo, z_down)
             spread("c0", z, y_lo, other_core)
 
-        def g2(k=k, spread=spread):
+        whole = SPREAD_MODE[k] == "A"
+
+        def g2(k=k, spread=spread, whole=whole):
             links.wait(("p1", k))
-            spread("p2", up(z, 3), y_lo, z_up, part=0)
+            spread("p2", up(z, 3), y_lo, z_up, part=None if whole else 0)
             links.wait(("m1", k))
-            spread("m2", up(z, 1), y_lo, z_down, part=1)
+            if not whole:
+                spread("m2", up(z, 1), y_lo, z_down, part=1)
+            spread("c1", up(z, 3), y_lo, other_core)
+            spread("c2", up(z, 1), y_lo, other_core)
+
+        def g5(k=k, spread=spread):
             links.wait(("y1", k))
             spread("p3", z, 1 - y_lo, z_up)
             spread("m3", z, 1 - y_lo, z_down)
-            spread("c1", up(z, 3), y_lo, other_core)
-            spread("c2", up(z, 1), y_lo, other_core)
             spread("c3", z, 1 - y_lo, other_core)
 
-        def g3(k=k, spread=spread):
-            links.wait(("p2", k), ("m2", k))
-            spread("y3", up(z, 2), y_lo, y_across)
-            spread("c4", up(z, 2), y_lo, other_core)
-
-        def g4(k=k, spread=spread):
-            links.wait(("p3", k), ("m3", k))
+        def g3(k=k, spread=spread, whole=whole):
+            if whole:
+                links.wait(("m3", k))
+                spread("m2", up(z, 1), 1 - y_lo, z_down)
+                spread("c4", up(z, 1), 1 - y_lo, other_core)
+            else:
+                links.wait(("p2", k), ("m2", k))
+                spread("y3", up(z, 2), y_lo, y_across)
+                spread("c4", up(z, 2), y_lo, other_core)
+
+        def g4(k=k, spread=spread, whole=whole):
+            links.wait(("p3", k))
             spread("c5", up(z, 3), 1 - y_lo, other_core)
-            spread("c6", up(z, 1), 1 - y_lo, other_core)
-            links.wait(("y3", k))
+            if whole:
+                links.wait(("p2", k))
+                spread("c6", up(z, 2), y_lo, other_core)
+                links.wait(("m2", k))
+            else:
+                links.wait(("m3", k))
+                spread("c6", up(z, 1), 1 - y_lo, other_core)
+                links.wait(("y3", k))
             spread("c7", up(z, 2), 1 - y_lo, other_core)
 
         def weigh(k=k):
@@ -273,15 +321,17 @@
                 at = pl.ds(pl.multiple_of(i * block, block), block)
                 wt[k, :, at] = (full[k, at, :].T * w_ref[:, at]).astype(BF16)
 
-        steps["R1", k], steps["R2", k], steps["R3", k], steps["R4", k] = r1, second, third, r4
-        steps["G2", k], steps["G3", k], steps["G4", k], steps["W", k] = g2, g3, g4, weigh
+        steps["R2", k], steps["R3", k], steps["R4", k], steps["W", k] = second, third, r4, weigh
+        steps["G2", k], steps["G5", k], steps["G3", k], steps["G4", k] = g2, g5, g3, g4
+        if SUM_MODE[k] == "B":
+            steps["R5", k] = fourth
 
         for g in range(PARTS):
             def rows_of(dx, dy, k=k, g=g):
                 q = ((1 - y_hi) if dy else y_hi) * 4 + up(x, dx)
                 return chi.at[k, g, pl.ds(pl.multiple_of(q * rows_q, rows_q), rows_q)]
 
-            first, second, third, last = ring_sum(
+            first, second, third, fourth, last = ring_sum(
                 links, ("F", k, g), PANEL_MODE[k], rows_of, panel_in.at[k, g], x_up, x_down, hi_across, rows_q // 2
             )
 
@@ -294,22 +344,26 @@
                     dst = pl.ds(pl.multiple_of(i * tile, tile), tile)
                     chi[k, g, :, dst] = jnp.dot(wt[k], a_v[:, src], preferred_element_type=F32)
 
-                first()
+                for j in range(3):
+                    first(j)
 
             def f4(k=k, g=g, last=last):
                 chi_out[k * rows_q : (k + 1) * rows_q, g * cols : (g + 1) * cols] = last()
 
             steps["F1", k, g], steps["F2", k, g], steps["F3", k, g], steps["F4", k, g] = f1, second, third, f4
-
-    steps["A",] = lambda: product(0, 0, 8)
+            if PANEL_MODE[k] == "B":
+                steps["F5", k, g] = fourth
+
+    for j in range(4):
+        steps["A", j] = functools.partial(product, 0, j)
+        steps["L", j] = functools.partial(weights, j)
+        steps["B", j] = functools.partial(product, 1, j)
 
     def b0():
         choose(1)
-        product(1, 0, 2)
+        product(1, 0)
 
     steps["B", 0] = b0
-    for i in range(1, 4):
-        steps["B", i] = functools.partial(product, 1, 2 * i, 2 * i + 2)
 
     def s1():
         @pl.loop(0, 8)
@@ -357,25 +411,49 @@
             core_copy(k, j).wait_send()
 
 
+def hand_over(*arrays):
+    parts = 4
+
+    def kernel(*refs):
+        sources, targets, held = refs[: len(arrays)], refs[len(arrays) : 2 * len(arrays)], refs[2 * len(arrays) : -1]
+        sem = refs[-1]
+        copies = []
+        for n, (source, target, hold) in enumerate(zip(sources, targets, held)):
+            rows = source.shape[0] // parts
+            for i in range(parts):
+                at = pl.ds(i * rows, rows)
+                copies.append(
+                    (
+                        pltpu.make_async_copy(source.at[at], hold.at[at], sem.at[n, i, 0]),
+                        pltpu.make_async_copy(hold.at[at], target.at[at], sem.at[n, i, 1]),
+                    )
+                )
+        for load, _ in copies:
+            load.start()
+        for load, store in copies:
+            load.wait()
+            store.start()
+        for _, store in copies:
+            store.wait()
+
+    return pl.pallas_call(
+        kernel,
+        name="hand_over",
+        out_shape=tuple(jax.ShapeDtypeStruct(v.shape, v.dtype) for v in arrays),
+        in_specs=[pl.BlockSpec(memory_space=pl.ANY)] * len(arrays),
+        out_specs=tuple(pl.BlockSpec(memory_space=pl.ANY) for _ in arrays),
+        scratch_shapes=[pltpu.VMEM(v.shape, v.dtype) for v in arrays]
+        + [pltpu.SemaphoreType.DMA((len(arrays), parts, 2))],
+    )(*arrays)
+
+
 def body(pair_density, subspace, band_valence, band_conduction, occupied, energies):
     pairs, depth = pair_density.shape
     nb = subspace.shape[1]
-    total_pairs = pairs * lax.axis_size("pair")
-    band_table = jnp.stack([energies, occupied.astype(F32)], axis=1)
-    valence_rows = lookup(band_valence, band_table)
-    conduction_rows = lookup(band_conduction, band_table)
-    scale = 1.0 / math.sqrt(total_pairs)
-    pair_weight = (
-        -2.0
-        * valence_rows[:, 1]
-        * (1.0 - conduction_rows[:, 1])
-        / (jnp.abs(conduction_rows[:, 0] - valence_rows[:, 0]) + 0.5)
-        * scale
-    )
     width, own, rows_q, cols = nb // CHUNKS, pairs // 16, nb // CHUNKS // 8, depth // PARTS
     copies = CHUNKS * (8 + 8 + 8) + CHUNKS * PARTS * 8 + 7
     vmem, dma = pltpu.VMEM, pltpu.SemaphoreType.DMA
-    return pl.pallas_call(
+    chi_panel, subspace_chi = pl.pallas_call(
         kernel,
         name="project",
         out_shape=(
@@ -385,10 +463,11 @@
         in_specs=[
             pl.BlockSpec(memory_space=pl.ANY),
             pl.BlockSpec(memory_space=pl.ANY),
-            pl.BlockSpec(memory_space=vmem),
-        ],
+        ]
+        + [pl.BlockSpec(memory_space=vmem)] * 4,
         out_specs=(pl.BlockSpec(memory_space=vmem), pl.BlockSpec(memory_space=vmem)),
         scratch_shapes=[
+            vmem((1, pairs), F32),
             vmem((pairs, depth), BF16),
             vmem((depth, nb), BF16),
             vmem((depth, 2 * width), BF16),
@@ -410,7 +489,8 @@
         compiler_params=pltpu.CompilerParams(
             collective_id=0, has_side_effects=True, vmem_limit_bytes=67043328
         ),
-    )(pair_density, subspace, pair_weight[None, :])
+    )(pair_density, subspace, band_valence[None, :], band_conduction[None, :], occupied[None, :], energies[None, :])
+    return hand_over(chi_panel, subspace_chi)
 
 
 def solution(mesh):

time: 130 us -> 105 us (0.81)
  Pallas kernels: 116 us -> 104 us
  matrix products: 7.91 us -> 0 us
  local copies, waits for them, and re-layouts: 3.39 us -> 0 us
  other arithmetic: 1.35 us -> 0 us
    pallas_call x1, Pallas kernels: 116 us -> 102 us  [body(): pl.pallas_call(kernel, name='project', out_shape=(jax.ShapeDtypeStruct((n...]
    dot_general x2 -> x0, matrix products: 7.91 us -> none  [lookup(): return jnp.dot(one_hot, table, precision=lax.Precision.HIGHEST)]
    unnamed x2 -> x0, local copies, waits for them, and re-layouts: 3.39 us -> none
    pallas_call x0 -> x1, Pallas kernels: none -> 2.04 us  [hand_over(): pl.pallas_call(kernel, name='hand_over', out_shape=tuple((jax.ShapeDtypeS...]
where the time goes in v2:
time: 105 us
  Pallas kernels  104 us (99%)
    pallas_call x1, Pallas kernels, body(): pl.pallas_call(kernel, name='project', out_shape=(jax.ShapeDtypeStruct((n...  102 us

profile of v2, /device:TPU:0, one launch (start us, length us, event | category | flops | bytes accessed | tf_op | source)
XLA Modules:
  0.0 105.0 jit_solution(11337510661342731940)
XLA Ops:
  0.6 102.2 %project.1 = (f32[64,3072]{1,0:T(8,128)}, f32[32,64]{1,0:T(8,128)}) custom-call(bf16[3072,3072]{1,0:T(8,128)(2,1)} %a_hbm.1, bf16[3072,512]{1,0:T(8,128)(2,1)} %s_hbm.1, s32[1,3072]{1,0:T(1,128)} %bitcast.4, s32[1,3072]{1,0:T(1,128)} %bitcast.5, s32[1,512]{1,0:T(1,128)} %bitcast.6, f32[1,512]{1,0:T(1,128)} %bitcast.7), custom_call_target="tpu_custom_call" | custom-call | tf_op jit(solution)/shard_map/project/pallas_call | solution.py:456
  102.8 2.0 %hand_over.1 = (f32[64,3072]{1,0:T(8,128)}, f32[32,64]{1,0:T(8,128)}) custom-call(f32[64,3072]{1,0:T(8,128)} %get-tuple-element.4.refs_0_, f32[32,64]{1,0:T(8,128)} %get-tuple-element.5.refs_1_), custom_call_target="tpu_custom_call" | custom-call | tf_op jit(solution)/shard_map/hand_over/pallas_call | solution.py:439

commit v3 on v2

v3 whole, which is shorter than its diff:
```python
import functools
import math

import jax
import jax.numpy as jnp
from jax import lax
from jax.experimental import pallas as pl
from jax.experimental.pallas import tpu as pltpu
from jax.sharding import PartitionSpec as P

MESH = pl.DeviceIdType.MESH
F32, BF16 = jnp.float32, jnp.bfloat16

CHUNKS = 4
PARTS = 2
SUM_MODE = "BABB"
SPREAD_MODE = "BBBB"
PANEL_MODE = "ABBBBBBB"
ORDER = (
    ("A", 0), ("A", 1), ("Q", 0, 0), ("Q", 1, 0), ("A", 2), ("Q", 0, 1), ("Q", 1, 1), ("Q", 0, 2),
    ("A", 3), ("Q", 0, 3), ("R2", 0), ("Q", 1, 2), ("B", 0), ("Q", 1, 3), ("R2", 1), ("B", 1),
    ("R3", 0), ("R5", 0), ("B", 2), ("Q", 2, 0), ("L", 1), ("Q", 2, 1), ("Q", 2, 2), ("L", 3),
    ("R3", 1), ("R4", 0), ("B", 3), ("R4", 1), ("Q", 3, 0), ("L", 0), ("G2", 0), ("L", 2),
    ("Q", 2, 3), ("G5", 0), ("R2", 2), ("G2", 1), ("G3", 0), ("Q", 3, 1), ("Q", 3, 2), ("Q", 3, 3),
    ("R2", 3), ("G5", 1), ("R3", 2), ("G4", 0), ("R5", 2), ("G3", 1), ("W", 0), ("F1", 0, 0),
    ("R3", 3), ("F1", 0, 1), ("R5", 3), ("G4", 1), ("W", 1), ("R4", 2), ("F1", 1, 0), ("R4", 3),
    ("F1", 1, 1), ("F2", 0, 1), ("G2", 2), ("G5", 2), ("F2", 0, 0), ("F2", 1, 0), ("G2", 3), ("G3", 2),
    ("F3", 1, 0), ("G5", 3), ("F5", 0, 1), ("F2", 1, 1), ("G3", 3), ("F3", 0, 0), ("G4", 2), ("F5", 1, 0),
    ("W", 2), ("F1", 2, 0), ("F5", 1, 1), ("G4", 3), ("F1", 2, 1), ("W", 3), ("F1", 3, 0), ("F1", 3, 1),
    ("F3", 0, 1), ("F3", 1, 1), ("S1",), ("F4", 0, 0), ("F2", 2, 0), ("F2", 2, 1), ("F2", 3, 0), ("F3", 2, 1),
    ("F2", 3, 1), ("F3", 3, 0), ("F3", 3, 1), ("F5", 2, 0), ("F5", 2, 1), ("S2",), ("F3", 2, 0), ("F5", 3, 1),
    ("F4", 1, 0), ("F5", 3, 0), ("F4", 2, 1), ("F4", 1, 1), ("F4", 2, 0), ("F4", 0, 1), ("F4", 3, 1), ("F4", 3, 0),
)


class Links:
    def __init__(self, send_sem, recv_sem, device):
        self.send_sem, self.recv_sem, self.device = send_sem, recv_sem, device
        self.sent, self.received, self.size = {}, {}, {}

    def send(self, send_group, group, source, target, device):
        out = self.sent.setdefault(send_group, len(self.sent))
        back = self.received.setdefault(group, len(self.received))
        pltpu.make_async_remote_copy(
            source, target, self.send_sem.at[out], self.recv_sem.at[back], device_id=device, device_id_type=MESH
        ).start()
        amount = math.prod(source.shape)
        self.size["s", send_group] = self.size.get(("s", send_group), 0) + amount
        self.size["r", group] = self.size.get(("r", group), 0) + amount

    def _all(self, kind, group, at, ref):
        assert math.prod(ref.shape) == self.size[kind, group], group
        return pltpu.make_async_remote_copy(
            ref, ref, self.send_sem.at[at if kind == "s" else 0], self.recv_sem.at[at if kind == "r" else 0],
            device_id=self.device, device_id_type=MESH,
        )

    def wait(self, group, ref):
        self._all("r", group, self.received[group], ref).wait_recv()

    def finish(self, group, ref):
        self._all("s", group, self.sent[group], ref).wait_send()


def ring_sum(links, tag, mode, piece, slots, ring_up, ring_down, across, half):
    lo, hi = pl.ds(0, half), pl.ds(half, half)

    def add(ref, *others):
        total = ref[...]
        for other in others:
            total = total + other[...]
        ref[...] = total

    def send(group, source, slot, device):
        links.send(tag, (tag, group), source, slot, device)

    def wait(group, ref):
        links.wait((tag, group), ref)

    def first(j):
        if mode == "B":
            if j == 0:
                send("a", piece(2, 1), slots.at[6], across)
            if j == 1:
                send("b", piece(1, 1), slots.at[0], ring_up)
            if j == 2:
                send("b", piece(3, 1), slots.at[1], ring_down)
        else:
            if j == 0:
                send("a", piece(2, 0), slots.at[2], ring_up)
                send("a", piece(2, 1), slots.at[3], ring_down)
            if j == 1:
                send("b", piece(1, 1), slots.at[0], ring_up)
            if j == 2:
                send("d", piece(3, 0), slots.at[1], ring_down)

    def second():
        if mode == "B":
            wait("a", slots.at[6])
            add(piece(2, 0), slots.at[6])
            send("c", piece(2, 0).at[lo], slots.at[2, lo], ring_up)
            send("c", piece(2, 0).at[hi], slots.at[3, hi], ring_down)
        else:
            wait("a", slots.at[pl.ds(2, 2)])
            add(piece(1, 0), slots.at[2])
            send("d", piece(1, 0), slots.at[4], ring_up)
            add(piece(3, 1), slots.at[3])
            send("b", piece(3, 1), slots.at[5], ring_down)

    def third():
        wait("b", slots.at[pl.ds(0, 2)])
        add(piece(0, 1), slots.at[0], slots.at[1 if mode == "B" else 5])
        send("d", piece(0, 1), slots.at[7], across)

    def fourth():
        wait("c", slots.at[2])
        add(piece(1, 0).at[lo], slots.at[2, lo])
        send("d", piece(1, 0), slots.at[4], ring_up)
        add(piece(3, 0).at[hi], slots.at[3, hi])
        send("d", piece(3, 0), slots.at[5], ring_down)

    def last():
        wait("d", slots.at[pl.ds(4, 3)])
        return piece(0, 0)[...] + slots[5 if mode == "B" else 1] + slots[4] + slots[7]

    return first, second, third, fourth, last


def kernel(
    a_hbm, s_hbm, valence_ref, conduction_ref, occupied_ref, energies_ref, chi_out, sub_out,
    w_ref, a_v, s_v, sp, coeff, core_in, sum_in, full, wt, chi, panel_in, sub_mine, sub_in,
    load_sem, core_send, core_recv, send_sem, recv_sem,
):
    pairs, depth = a_v.shape
    nb = s_v.shape[1]
    width = nb // CHUNKS
    block = pairs // 8
    own = block // 2
    rows_q = width // 8
    cols = depth // PARTS

    pair, slab = lax.axis_index("pair"), lax.axis_index("slab")
    y_hi, x = lax.div(pair, 4), lax.rem(pair, 4)
    y_lo, z, core = lax.div(slab, 8), lax.rem(lax.div(slab, 2), 4), lax.rem(slab, 2)

    def slab_of(y, zz, c):
        return (pair, y * 8 + zz * 2 + c)

    def pair_of(y, xx):
        return (y * 4 + xx, slab)

    def up(v, d):
        return lax.rem(v + d, 4)

    z_up, z_down = slab_of(y_lo, up(z, 1), core), slab_of(y_lo, up(z, 3), core)
    y_across, other_core = slab_of(1 - y_lo, z, core), slab_of(y_lo, z, 1 - core)
    x_up, x_down, hi_across = pair_of(y_hi, up(x, 1)), pair_of(y_hi, up(x, 3)), pair_of(1 - y_hi, x)

    def peer(d):
        return (lax.rem(pair + d, 8), slab)

    Z_ORDER = (2, 1, 3, 0)

    def block_rows(core_at, j):
        return pl.ds(pl.multiple_of((core_at * 4 + up(z, Z_ORDER[j])) * block, block), block)

    def half_rows(j):
        return pl.ds(pl.multiple_of(up(z, Z_ORDER[j]) * block, block), block)

    def side(i):
        return jnp.where(i == 0, 1 - core, core)

    def a_load(j, i):
        rows = block_rows(side(i), j)
        return pltpu.make_async_copy(a_hbm.at[rows], a_v.at[rows], load_sem.at[2 * j + i])

    barrier = pltpu.get_barrier_semaphore()
    greeted = [z_up, z_down, y_across, other_core] + [peer(d) for d in range(1, 8)]
    for device in greeted:
        pl.semaphore_signal(barrier, inc=1, device_id=device, device_id_type=MESH)

    def s_load(i):
        rows = pl.ds(pl.multiple_of(i * 2 * block, 2 * block), 2 * block)
        return pltpu.make_async_copy(s_hbm.at[rows], s_v.at[rows], load_sem.at[8 + i])

    for i in range(4):
        s_load(i).start()
    for j in range(4):
        for i in range(2):
            a_load(j, i).start()

    links = Links(send_sem, recv_sem, other_core)

    def pick(kp):
        to = lax.broadcasted_iota(jnp.int32, (1, 2 * width), 1)
        frm = lax.broadcasted_iota(jnp.int32, (nb, 2 * width), 0)
        k = kp * 2 + to // width
        b = (lax.rem(to, width) // rows_q) * (nb // 8) + k * rows_q + lax.rem(to, rows_q)
        return jnp.where(frm == b, 1.0, 0.0).astype(BF16)

    def choose(picked, loading):
        @pl.loop(0, 4)
        def _(i):
            if loading:
                s_load(i).wait()
            rows = pl.ds(pl.multiple_of(i * 2 * block, 2 * block), 2 * block)
            sp[rows, :] = jnp.dot(s_v[rows, :], picked, preferred_element_type=F32).astype(BF16)

    def core_copy(kp, j):
        two = pl.ds(2 * kp, 2)
        return pltpu.make_async_remote_copy(
            coeff.at[two, block_rows(1 - core, j)], core_in.at[two, half_rows(j)], core_send.at[kp], core_recv.at[kp, j],
            device_id=other_core, device_id_type=MESH,
        )

    def part_of_product(kp, j, i):
        rows = block_rows(side(i), j)
        if kp == 0:
            a_load(j, i).wait()
        part = jnp.dot(a_v[rows, :], sp[...], preferred_element_type=F32)
        for h in range(2):
            coeff[2 * kp + h, rows, :] = part[:, h * width : (h + 1) * width]

    def to_other_core(kp, j):
        core_copy(kp, j).start()

    def product(kp, j):
        @pl.loop(0, 2)
        def _(i):
            part_of_product(kp, j, i)

            @pl.when(i == 0)
            def _():
                to_other_core(kp, j)

    def weights(j):
        at = slice(j * (pairs // 4), (j + 1) * (pairs // 4))
        bands = energies_ref.shape[1]
        energy = energies_ref[...]
        high = energy.astype(BF16).astype(F32)
        middle = (energy - high).astype(BF16).astype(F32)
        low = energy - high - middle
        row = lax.broadcasted_iota(jnp.int32, (16, bands), 0)
        table = jnp.where(row == 0, high, jnp.where(row == 1, middle, jnp.where(row == 2, low, 0.0)))
        table = jnp.where(row == 3, occupied_ref[...].astype(F32), table).astype(BF16)
        band = lax.broadcasted_iota(jnp.int32, (bands, pairs // 4), 0)

        def lookup(indices):
            one_hot = jnp.where(band == indices, 1.0, 0.0).astype(BF16)
            found = jnp.dot(table, one_hot, preferred_element_type=F32)
            return found[0:1] + found[1:2] + found[2:3], found[3:4]

        energy_low, filled_low = lookup(valence_ref[:, at])
        energy_high, filled_high = lookup(conduction_ref[:, at])
        scale = 1.0 / math.sqrt(pairs * 8)
        w_ref[:, at] = -2.0 * filled_low * (1.0 - filled_high) / (jnp.abs(energy_high - energy_low) + 0.5) * scale

    def owner_rows(z_at, y_at):
        return pl.ds(pl.multiple_of((core * 4 + z_at) * block + y_at * own, own), own)

    steps = {}
    for k in range(CHUNKS):
        get = lambda dr, da, k=k: coeff.at[k, owner_rows(up(z, dr), (1 - y_lo) if da else y_lo)]
        first, second, third, fourth, last = ring_sum(
            links, ("R", k), SUM_MODE[k], get, sum_in.at[k], z_up, z_down, y_across, own // 2
        )

        def gather(j, k=k, first=first):
            if k % 2 == 0:
                core_copy(k // 2, j).wait_recv()
            here = block_rows(core, j)
            coeff[k, here, :] = coeff[k, here, :] + core_in[k, half_rows(j), :]
            first(j)

        for j in range(4):
            steps["Q", k, j] = functools.partial(gather, j)

        def spread(group, z_at, y_at, device, k=k, part=None):
            rows = owner_rows(z_at, y_at)
            if part is not None:
                start = (core * 4 + z_at) * block + y_at * own + part * (own // 2)
                rows = pl.ds(pl.multiple_of(start, own // 2), own // 2)
            links.send(("G", k), (group, k), full.at[k, rows], full.at[k, rows], device)

        def arrived(group, pieces, k=k):
            links.wait((group, k), full.at[k, pl.ds(0, pieces * own)])

        whole = SPREAD_MODE[k] == "A"

        def r4(k=k, last=last, spread=spread):
            full[k, owner_rows(z, y_lo), :] = last()
            spread("y", z, y_lo, y_across)
            spread("p", z, y_lo, z_up)
            spread("p", z, y_lo, z_down)
            spread("core", z, y_lo, other_core)

        def g2(spread=spread, arrived=arrived, whole=whole):
            arrived("p", 2)
            if whole:
                spread("l", up(z, 3), y_lo, z_up)
            else:
                spread("h", up(z, 3), y_lo, z_up, part=0)
                spread("h", up(z, 1), y_lo, z_down, part=1)
            spread("core", up(z, 3), y_lo, other_core)
            spread("core", up(z, 1), y_lo, other_core)

        def g5(spread=spread, arrived=arrived, whole=whole):
            arrived("y", 1)
            spread("l", z, 1 - y_lo, z_up)
            spread("h" if whole else "l", z, 1 - y_lo, z_down)
            spread("core", z, 1 - y_lo, other_core)

        def g3(spread=spread, arrived=arrived, whole=whole):
            arrived("h", 1)
            if whole:
                spread("l", up(z, 1), 1 - y_lo, z_down)
                spread("core", up(z, 1), 1 - y_lo, other_core)
            else:
                spread("l", up(z, 2), y_lo, y_across)
                spread("core", up(z, 2), y_lo, other_core)

        def weigh(core_at, k=k):
            for i in range(4):
                at = pl.ds(pl.multiple_of((core_at * 4 + i) * block, block), block)
                wt[k, :, at] = (full[k, at, :].T * w_ref[:, at]).astype(BF16)

        def g4(spread=spread, arrived=arrived, whole=whole, weigh=weigh):
            arrived("l", 3)
            spread("core", up(z, 3), 1 - y_lo, other_core)
            if whole:
                spread("core", up(z, 2), y_lo, other_core)
            else:
                spread("core", up(z, 1), 1 - y_lo, other_core)
            spread("core", up(z, 2), 1 - y_lo, other_core)
            weigh(core)

        def w1(arrived=arrived, weigh=weigh):
            arrived("core", 8)
            weigh(1 - core)

        steps["R2", k], steps["R3", k], steps["R4", k], steps["W", k] = second, third, r4, w1
        steps["G2", k], steps["G5", k], steps["G3", k], steps["G4", k] = g2, g5, g3, g4
        if SUM_MODE[k] == "B":
            steps["R5", k] = fourth

        for g in range(PARTS):
            def rows_of(dx, dy, k=k, g=g):
                q = ((1 - y_hi) if dy else y_hi) * 4 + up(x, dx)
                return chi.at[k, g, pl.ds(pl.multiple_of(q * rows_q, rows_q), rows_q)]

            first, second, third, fourth, last = ring_sum(
                links, ("F", k, g), PANEL_MODE[k * PARTS + g], rows_of, panel_in.at[k, g], x_up, x_down, hi_across, rows_q // 2
            )

            def f1(k=k, g=g, first=first):
                tile = cols // 3

                @pl.loop(0, 3)
                def _(i):
                    src = pl.ds(pl.multiple_of(g * cols + i * tile, tile), tile)
                    dst = pl.ds(pl.multiple_of(i * tile, tile), tile)
                    chi[k, g, :, dst] = jnp.dot(wt[k], a_v[:, src], preferred_element_type=F32)

                for j in range(3):
                    first(j)

            def f4(k=k, g=g, last=last):
                chi_out[k * rows_q : (k + 1) * rows_q, g * cols : (g + 1) * cols] = last()

            steps["F1", k, g], steps["F2", k, g], steps["F3", k, g], steps["F4", k, g] = f1, second, third, f4
            if PANEL_MODE[k * PARTS + g] == "B":
                steps["F5", k, g] = fourth

    for j in range(4):
        steps["A", j] = functools.partial(product, 0, j)
        steps["L", j] = functools.partial(weights, j)
        steps["B", j] = functools.partial(product, 1, j)

    def a0():
        part_of_product(0, 0, 0)
        pl.semaphore_wait(barrier, len(greeted))
        to_other_core(0, 0)
        part_of_product(0, 0, 1)

    def b0():
        choose(pick(1), False)
        product(1, 0)

    steps["A", 0], steps["B", 0] = a0, b0

    def s1():
        @pl.loop(0, 8)
        def _(i):
            at = pl.ds(pl.multiple_of(i * block, block), block)
            for h in range(2):
                value = full[2 * core + h, at, :]
                high = value.astype(BF16)
                s_v[at, 2 * h * width : (2 * h + 1) * width] = high
                s_v[at, (2 * h + 1) * width : (2 * h + 2) * width] = (value - high.astype(F32)).astype(BF16)

        q = lax.div(slab, 2)
        lane = lax.broadcasted_iota(jnp.int32, (width, width), 1)
        for k in range(CHUNKS):
            part = jnp.dot(wt[k], s_v[...], preferred_element_type=F32)
            even = part[:, :width] + part[:, width : 2 * width]
            odd = part[:, 2 * width : 3 * width] + part[:, 3 * width :]
            even = pltpu.roll(even, lax.rem(width - q * rows_q, width), 1)
            odd = pltpu.roll(odd, lax.rem(width + rows_q - q * rows_q, width), 1)
            mine = jnp.where(lane < rows_q, even, jnp.where(lane < 2 * rows_q, odd, 0.0))
            for o in range(8):
                sub_mine[o, k * rows_q : (k + 1) * rows_q, :] = mine[o * rows_q : (o + 1) * rows_q]
        for d in range(1, 8):
            links.send("s", "s", sub_mine.at[lax.rem(pair + d, 8)], sub_in.at[d - 1], peer(d))

    def s2():
        total = sub_mine[pair]
        links.wait("s", sub_in)
        for d in range(1, 8):
            total = total + sub_in[d - 1]
        square = jnp.concatenate([total, jnp.zeros_like(total)], axis=0)
        sub_out[...] = square.T[: 2 * rows_q, : 4 * rows_q]

    steps["S1",], steps["S2",] = s1, s2

    picked = pick(0)
    choose(picked, True)
    assert sorted(ORDER, key=str) == sorted(steps, key=str)
    for name in ORDER:
        steps[name]()
    for k in range(CHUNKS):
        links.finish(("R", k), sum_in.at[k, pl.ds(0, 7)])
        links.finish(("G", k), full.at[k, pl.ds(0, 15 * own)])
        for g in range(PARTS):
            links.finish(("F", k, g), panel_in.at[k, g, pl.ds(0, 7)])
    links.finish("s", sub_in)
    for kp in range(CHUNKS // 2):
        two = pl.ds(2 * kp, 2)
        pltpu.make_async_remote_copy(
            core_in.at[two], core_in.at[two], core_send.at[kp], core_recv.at[kp, 0],
            device_id=other_core, device_id_type=MESH,
        ).wait_send()


def hand_over(*arrays):
    def kernel(*refs):
        sources, targets, sem = refs[: len(arrays)], refs[len(arrays) : 2 * len(arrays)], refs[-1]
        copies = [
            pltpu.make_async_copy(source, target, sem.at[n])
            for n, (source, target) in enumerate(zip(sources, targets))
        ]
        for copy in copies:
            copy.start()
        for copy in copies:
            copy.wait()

    return pl.pallas_call(
        kernel,
        name="hand_over",
        out_shape=tuple(jax.ShapeDtypeStruct(v.shape, v.dtype) for v in arrays),
        in_specs=[pl.BlockSpec(memory_space=pltpu.VMEM)] * len(arrays),
        out_specs=tuple(pl.BlockSpec(memory_space=pl.ANY) for _ in arrays),
        scratch_shapes=[pltpu.SemaphoreType.DMA((len(arrays),))],
        compiler_params=pltpu.CompilerParams(vmem_limit_bytes=1 << 20),
    )(*arrays)


def body(pair_density, subspace, band_valence, band_conduction, occupied, energies):
    pairs, depth = pair_density.shape
    nb = subspace.shape[1]
    width, own, rows_q, cols = nb // CHUNKS, pairs // 16, nb // CHUNKS // 8, depth // PARTS
    vmem, dma = pltpu.VMEM, pltpu.SemaphoreType.DMA
    chi_panel, subspace_chi = pl.pallas_call(
        kernel,
        name="project",
        out_shape=(
            pltpu.VMEM((nb // 8, depth), F32),
            pltpu.VMEM((nb // 16, nb // 8), F32),
        ),
        in_specs=[
            pl.BlockSpec(memory_space=pl.ANY),
            pl.BlockSpec(memory_space=pl.ANY),
        ]
        + [pl.BlockSpec(memory_space=vmem)] * 4,
        out_specs=(pl.BlockSpec(memory_space=vmem), pl.BlockSpec(memory_space=vmem)),
        scratch_shapes=[
            vmem((1, pairs), F32),
            vmem((pairs, depth), BF16),
            vmem((depth, nb), BF16),
            vmem((depth, 2 * width), BF16),
            vmem((CHUNKS, pairs, width), F32),
            vmem((CHUNKS, pairs // 2, width), F32),
            vmem((CHUNKS, 8, own, width), F32),
            vmem((CHUNKS, pairs, width), F32),
            vmem((CHUNKS, width, pairs), BF16),
            vmem((CHUNKS, PARTS, width, cols), F32),
            vmem((CHUNKS, PARTS, 8, rows_q, cols), F32),
            vmem((8, nb // 8, width), F32),
            vmem((7, nb // 8, width), F32),
            dma((12,)),
            dma((CHUNKS // 2,)),
            dma((CHUNKS // 2, 4)),
            dma((CHUNKS * (2 + PARTS) + 1,)),
            dma((CHUNKS * (4 + 5) + CHUNKS * PARTS * 4 + 1,)),
        ],
        compiler_params=pltpu.CompilerParams(
            collective_id=0, has_side_effects=True, vmem_limit_bytes=62500000
        ),
    )(pair_density, subspace, band_valence[None, :], band_conduction[None, :], occupied[None, :], energies[None, :])
    return hand_over(chi_panel, subspace_chi)


def solution(mesh):
    return jax.shard_map(
        body,
        mesh=mesh,
        in_specs=(P("pair", "slab"), P("slab", None), P("pair"), P("pair"), P(), P()),
        out_specs=(P("pair", "slab"), P("slab", "pair")),
        check_vma=False,
    )
```

time: 105 us -> 95.4 us (0.909)
  Pallas kernels: 104 us -> 93.6 us
    pallas_call x1, Pallas kernels: 102 us -> 92.7 us  [body(): pl.pallas_call(kernel, name='project', out_shape=(pltpu.VMEM((nb // 8, de...]
    pallas_call x1, Pallas kernels: 2.04 us -> 0.9 us  [hand_over(): pl.pallas_call(kernel, name='hand_over', out_shape=tuple((jax.ShapeDtypeS...]
where the time goes in v3:
time: 95.4 us; the launch traced here: 94.4 us
  Pallas kernels  93.6 us (98%)
    pallas_call x1, Pallas kernels, body(): pl.pallas_call(kernel, name='project', out_shape=(pltpu.VMEM((nb // 8, de...  92.7 us

profile of v3, /device:TPU:0, one launch (start us, length us, event | category | flops | bytes accessed | tf_op | source)
XLA Modules:
  0.0 94.4 jit_solution(5378390374744283810)
XLA Ops:
  0.6 92.7 %project.1 = (f32[64,3072]{1,0:T(8,128)S(1)}, f32[32,64]{1,0:T(8,128)S(1)}) custom-call(bf16[3072,3072]{1,0:T(8,128)(2,1)} %a_hbm.1, bf16[3072,512]{1,0:T(8,128)(2,1)} %s_hbm.1, s32[1,3072]{1,0:T(1,128)} %bitcast.4, s32[1,3072]{1,0:T(1,128)} %bitcast.5, s32[1,512]{1,0:T(1,128)} %bitcast.6, f32[1,512]{1,0:T(1,128)} %bitcast.7), custom_call_target="tpu_custom_call" | custom-call | tf_op jit(solution)/shard_map/project/pallas_call | solution.py:472
  93.3 0.9 hand_over.1

commit v4 on v3

--- a/solution.py
+++ b/solution.py
@@ -12,24 +12,31 @@
 F32, BF16 = jnp.float32, jnp.bfloat16
 
 CHUNKS = 4
-PARTS = 2
+TILE = 512
+PARTS = 3
 SUM_MODE = "BABB"
 SPREAD_MODE = "BBBB"
-PANEL_MODE = "ABBBBBBB"
+PANEL_MODE = "BBABBBBBBBBB"
 ORDER = (
-    ("A", 0), ("A", 1), ("Q", 0, 0), ("Q", 1, 0), ("A", 2), ("Q", 0, 1), ("Q", 1, 1), ("Q", 0, 2),
-    ("A", 3), ("Q", 0, 3), ("R2", 0), ("Q", 1, 2), ("B", 0), ("Q", 1, 3), ("R2", 1), ("B", 1),
-    ("R3", 0), ("R5", 0), ("B", 2), ("Q", 2, 0), ("L", 1), ("Q", 2, 1), ("Q", 2, 2), ("L", 3),
-    ("R3", 1), ("R4", 0), ("B", 3), ("R4", 1), ("Q", 3, 0), ("L", 0), ("G2", 0), ("L", 2),
-    ("Q", 2, 3), ("G5", 0), ("R2", 2), ("G2", 1), ("G3", 0), ("Q", 3, 1), ("Q", 3, 2), ("Q", 3, 3),
-    ("R2", 3), ("G5", 1), ("R3", 2), ("G4", 0), ("R5", 2), ("G3", 1), ("W", 0), ("F1", 0, 0),
-    ("R3", 3), ("F1", 0, 1), ("R5", 3), ("G4", 1), ("W", 1), ("R4", 2), ("F1", 1, 0), ("R4", 3),
-    ("F1", 1, 1), ("F2", 0, 1), ("G2", 2), ("G5", 2), ("F2", 0, 0), ("F2", 1, 0), ("G2", 3), ("G3", 2),
-    ("F3", 1, 0), ("G5", 3), ("F5", 0, 1), ("F2", 1, 1), ("G3", 3), ("F3", 0, 0), ("G4", 2), ("F5", 1, 0),
-    ("W", 2), ("F1", 2, 0), ("F5", 1, 1), ("G4", 3), ("F1", 2, 1), ("W", 3), ("F1", 3, 0), ("F1", 3, 1),
-    ("F3", 0, 1), ("F3", 1, 1), ("S1",), ("F4", 0, 0), ("F2", 2, 0), ("F2", 2, 1), ("F2", 3, 0), ("F3", 2, 1),
-    ("F2", 3, 1), ("F3", 3, 0), ("F3", 3, 1), ("F5", 2, 0), ("F5", 2, 1), ("S2",), ("F3", 2, 0), ("F5", 3, 1),
-    ("F4", 1, 0), ("F5", 3, 0), ("F4", 2, 1), ("F4", 1, 1), ("F4", 2, 0), ("F4", 0, 1), ("F4", 3, 1), ("F4", 3, 0),
+    ("A", 0), ("A", 1), ("Q", 0, 0), ("Q", 1, 0), ("A", 2), ("L", 0), ("Q", 0, 1), ("Q", 0, 2),
+    ("A", 3), ("Q", 0, 3), ("R2", 0), ("Q", 1, 1), ("Q", 1, 2), ("L", 2), ("Q", 1, 3), ("R2", 1),
+    ("C",), ("B", 0), ("R5", 0), ("R3", 0), ("B", 1), ("Q", 2, 0), ("B", 2), ("Q", 2, 1),
+    ("L", 3), ("Q", 2, 2), ("R3", 1), ("L", 1), ("R4", 0), ("B", 3), ("R4", 1), ("Q", 2, 3),
+    ("R2", 2), ("G2", 0), ("G5", 0), ("Q", 3, 0), ("G2", 1), ("G5", 1), ("R5", 2), ("G3", 0),
+    ("R3", 2), ("Q", 3, 1), ("Q", 3, 2), ("G4", 0), ("Q", 3, 3), ("V", 0), ("R2", 3), ("G3", 1),
+    ("W", 0), ("F0", 0, 1, 0), ("F1", 0, 1), ("F0", 0, 2, 0), ("R4", 2), ("F1", 0, 2), ("G4", 1), ("V", 1),
+    ("R3", 3), ("F0", 0, 0, 0), ("F1", 0, 0), ("R5", 3), ("W", 1), ("F0", 1, 1, 0), ("F1", 1, 1), ("G2", 2),
+    ("F0", 1, 2, 0), ("F0", 1, 0, 0), ("F2", 0, 2), ("F2", 0, 1), ("F1", 1, 0), ("R4", 3), ("F1", 1, 2), ("G5", 2),
+    ("F2", 1, 1), ("G3", 2), ("F2", 0, 0), ("F2", 1, 0), ("F3", 1, 0), ("F3", 0, 2), ("F5", 0, 1), ("G2", 3),
+    ("F5", 1, 1), ("F2", 1, 2), ("G5", 3), ("F5", 0, 0), ("F5", 1, 0), ("G4", 2), ("G3", 3), ("V", 2),
+    ("W", 2), ("F0", 2, 0, 0), ("F1", 2, 0), ("F0", 2, 2, 0), ("F5", 1, 2), ("F0", 2, 1, 0), ("F1", 2, 2), ("F1", 2, 1),
+    ("G4", 3), ("V", 3), ("F3", 1, 1), ("W", 3), ("F0", 3, 2, 0), ("F1", 3, 2), ("F0", 3, 0, 0), ("F3", 0, 1),
+    ("F2", 2, 2), ("F0", 3, 1, 0), ("F2", 2, 0), ("S0",), ("F1", 3, 1), ("F2", 2, 1), ("S", 0), ("F1", 3, 0),
+    ("F3", 2, 2), ("S", 1), ("F3", 1, 2), ("S", 2), ("F3", 2, 1), ("F3", 2, 0), ("F4", 0, 2), ("F5", 2, 0),
+    ("S", 3), ("F2", 3, 2), ("F4", 0, 1), ("F2", 3, 1), ("F4", 1, 1), ("S1",), ("F5", 2, 1), ("F2", 3, 0),
+    ("F3", 3, 1), ("F3", 3, 0), ("S2",), ("F5", 2, 2), ("F3", 3, 2), ("F5", 3, 1), ("F4", 1, 0), ("F5", 3, 2),
+    ("F5", 3, 0), ("S3",), ("F4", 2, 1), ("F3", 0, 0), ("S4",), ("F4", 1, 2), ("F4", 2, 2), ("F4", 2, 0),
+    ("F4", 0, 0), ("F4", 3, 1), ("F4", 3, 2), ("F4", 3, 0),
 )
 
 
@@ -156,9 +163,6 @@
     y_across, other_core = slab_of(1 - y_lo, z, core), slab_of(y_lo, z, 1 - core)
     x_up, x_down, hi_across = pair_of(y_hi, up(x, 1)), pair_of(y_hi, up(x, 3)), pair_of(1 - y_hi, x)
 
-    def peer(d):
-        return (lax.rem(pair + d, 8), slab)
-
     Z_ORDER = (2, 1, 3, 0)
 
     def block_rows(core_at, j):
@@ -175,7 +179,7 @@
         return pltpu.make_async_copy(a_hbm.at[rows], a_v.at[rows], load_sem.at[2 * j + i])
 
     barrier = pltpu.get_barrier_semaphore()
-    greeted = [z_up, z_down, y_across, other_core] + [peer(d) for d in range(1, 8)]
+    greeted = [other_core, z_up, z_down, y_across, x_up, x_down, hi_across]
     for device in greeted:
         pl.semaphore_signal(barrier, inc=1, device_id=device, device_id_type=MESH)
 
@@ -231,6 +235,8 @@
 
             @pl.when(i == 0)
             def _():
+                if kp == 0 and j == 0:
+                    pl.semaphore_wait(barrier, len(greeted))
                 to_other_core(kp, j)
 
     def weights(j):
@@ -324,7 +330,7 @@
                 at = pl.ds(pl.multiple_of((core_at * 4 + i) * block, block), block)
                 wt[k, :, at] = (full[k, at, :].T * w_ref[:, at]).astype(BF16)
 
-        def g4(spread=spread, arrived=arrived, whole=whole, weigh=weigh):
+        def g4(spread=spread, arrived=arrived, whole=whole):
             arrived("l", 3)
             spread("core", up(z, 3), 1 - y_lo, other_core)
             if whole:
@@ -332,7 +338,6 @@
             else:
                 spread("core", up(z, 1), 1 - y_lo, other_core)
             spread("core", up(z, 2), 1 - y_lo, other_core)
-            weigh(core)
 
         def w1(arrived=arrived, weigh=weigh):
             arrived("core", 8)
@@ -340,6 +345,7 @@
 
         steps["R2", k], steps["R3", k], steps["R4", k], steps["W", k] = second, third, r4, w1
         steps["G2", k], steps["G5", k], steps["G3", k], steps["G4", k] = g2, g5, g3, g4
+        steps["V", k] = functools.partial(weigh, core)
         if SUM_MODE[k] == "B":
             steps["R5", k] = fourth
 
@@ -352,17 +358,17 @@
                 links, ("F", k, g), PANEL_MODE[k * PARTS + g], rows_of, panel_in.at[k, g], x_up, x_down, hi_across, rows_q // 2
             )
 
-            def f1(k=k, g=g, first=first):
-                tile = cols // 3
-
-                @pl.loop(0, 3)
-                def _(i):
-                    src = pl.ds(pl.multiple_of(g * cols + i * tile, tile), tile)
-                    dst = pl.ds(pl.multiple_of(i * tile, tile), tile)
-                    chi[k, g, :, dst] = jnp.dot(wt[k], a_v[:, src], preferred_element_type=F32)
-
+            def tile(i, k=k, g=g):
+                src, dst = pl.ds(g * cols + i * TILE, TILE), pl.ds(i * TILE, TILE)
+                chi[k, g, :, dst] = jnp.dot(wt[k], a_v[:, src], preferred_element_type=F32)
+
+            def f1(tile=tile, first=first):
+                tile(cols // TILE - 1)
                 for j in range(3):
                     first(j)
+
+            for i in range(cols // TILE - 1):
+                steps["F0", k, g, i] = functools.partial(tile, i)
 
             def f4(k=k, g=g, last=last):
                 chi_out[k * rows_q : (k + 1) * rows_q, g * cols : (g + 1) * cols] = last()
@@ -375,52 +381,47 @@
         steps["A", j] = functools.partial(product, 0, j)
         steps["L", j] = functools.partial(weights, j)
         steps["B", j] = functools.partial(product, 1, j)
-
-    def a0():
-        part_of_product(0, 0, 0)
-        pl.semaphore_wait(barrier, len(greeted))
-        to_other_core(0, 0)
-        part_of_product(0, 0, 1)
-
-    def b0():
-        choose(pick(1), False)
-        product(1, 0)
-
-    steps["A", 0], steps["B", 0] = a0, b0
-
-    def s1():
-        @pl.loop(0, 8)
-        def _(i):
-            at = pl.ds(pl.multiple_of(i * block, block), block)
+    steps["C",] = lambda: choose(pick(1), False)
+
+    first, second, third, _, last = ring_sum(
+        links, "S", "A",
+        lambda dx, dy: sub_mine.at[((1 - y_hi) if dy else y_hi) * 4 + up(x, dx)],
+        sub_in, x_up, x_down, hi_across, 0,
+    )
+
+    def s0():
+        for i in range(8):
+            at = pl.ds(i * block, block)
             for h in range(2):
                 value = full[2 * core + h, at, :]
                 high = value.astype(BF16)
                 s_v[at, 2 * h * width : (2 * h + 1) * width] = high
                 s_v[at, (2 * h + 1) * width : (2 * h + 2) * width] = (value - high.astype(F32)).astype(BF16)
 
+    def s(k):
         q = lax.div(slab, 2)
         lane = lax.broadcasted_iota(jnp.int32, (width, width), 1)
-        for k in range(CHUNKS):
-            part = jnp.dot(wt[k], s_v[...], preferred_element_type=F32)
-            even = part[:, :width] + part[:, width : 2 * width]
-            odd = part[:, 2 * width : 3 * width] + part[:, 3 * width :]
-            even = pltpu.roll(even, lax.rem(width - q * rows_q, width), 1)
-            odd = pltpu.roll(odd, lax.rem(width + rows_q - q * rows_q, width), 1)
-            mine = jnp.where(lane < rows_q, even, jnp.where(lane < 2 * rows_q, odd, 0.0))
-            for o in range(8):
-                sub_mine[o, k * rows_q : (k + 1) * rows_q, :] = mine[o * rows_q : (o + 1) * rows_q]
-        for d in range(1, 8):
-            links.send("s", "s", sub_mine.at[lax.rem(pair + d, 8)], sub_in.at[d - 1], peer(d))
-
-    def s2():
-        total = sub_mine[pair]
-        links.wait("s", sub_in)
-        for d in range(1, 8):
-            total = total + sub_in[d - 1]
+        part = jnp.dot(wt[k], s_v[...], preferred_element_type=F32)
+        even = part[:, :width] + part[:, width : 2 * width]
+        odd = part[:, 2 * width : 3 * width] + part[:, 3 * width :]
+        even = pltpu.roll(even, lax.rem(width - q * rows_q, width), 1)
+        odd = pltpu.roll(odd, lax.rem(width + rows_q - q * rows_q, width), 1)
+        mine = jnp.where(lane < rows_q, even, jnp.where(lane < 2 * rows_q, odd, 0.0))
+        for o in range(8):
+            sub_mine[o, k * rows_q : (k + 1) * rows_q, :] = mine[o * rows_q : (o + 1) * rows_q]
+
+    def s1():
+        for j in range(3):
+            first(j)
+
+    def s4():
+        total = last()
         square = jnp.concatenate([total, jnp.zeros_like(total)], axis=0)
         sub_out[...] = square.T[: 2 * rows_q, : 4 * rows_q]
 
-    steps["S1",], steps["S2",] = s1, s2
+    steps["S0",], steps["S1",], steps["S2",], steps["S3",], steps["S4",] = s0, s1, second, third, s4
+    for k in range(CHUNKS):
+        steps["S", k] = functools.partial(s, k)
 
     picked = pick(0)
     choose(picked, True)
@@ -432,7 +433,7 @@
         links.finish(("G", k), full.at[k, pl.ds(0, 15 * own)])
         for g in range(PARTS):
             links.finish(("F", k, g), panel_in.at[k, g, pl.ds(0, 7)])
-    links.finish("s", sub_in)
+    links.finish("S", sub_in.at[pl.ds(0, 7)])
     for kp in range(CHUNKS // 2):
         two = pl.ds(2 * kp, 2)
         pltpu.make_async_remote_copy(
@@ -495,12 +496,12 @@
             vmem((CHUNKS, PARTS, width, cols), F32),
             vmem((CHUNKS, PARTS, 8, rows_q, cols), F32),
             vmem((8, nb // 8, width), F32),
-            vmem((7, nb // 8, width), F32),
+            vmem((8, nb // 8, width), F32),
             dma((12,)),
             dma((CHUNKS // 2,)),
             dma((CHUNKS // 2, 4)),
             dma((CHUNKS * (2 + PARTS) + 1,)),
-            dma((CHUNKS * (4 + 5) + CHUNKS * PARTS * 4 + 1,)),
+            dma((CHUNKS * (4 + 5) + CHUNKS * PARTS * 4 + 3,)),
         ],
         compiler_params=pltpu.CompilerParams(
             collective_id=0, has_side_effects=True, vmem_limit_bytes=62500000

time: 95.4 us -> 92.3 us (0.968)
  Pallas kernels: 93.6 us -> 91.3 us
    pallas_call x1, Pallas kernels: 92.7 us -> 90.4 us  [body(): pl.pallas_call(kernel, name='project', out_shape=(pltpu.VMEM((nb // 8, de...]
where the time goes in v4:
time: 92.3 us; the launch traced here: 92.2 us
  Pallas kernels  91.3 us (99%)
    pallas_call x1, Pallas kernels, body(): pl.pallas_call(kernel, name='project', out_shape=(pltpu.VMEM((nb // 8, de...  90.4 us

profile of v4, /device:TPU:0, one launch (start us, length us, event | category | flops | bytes accessed | tf_op | source)
XLA Modules:
  0.0 92.2 jit_solution(7542767449559204855)
XLA Ops:
  0.6 90.4 %project.1 = (f32[64,3072]{1,0:T(8,128)S(1)}, f32[32,64]{1,0:T(8,128)S(1)}) custom-call(bf16[3072,3072]{1,0:T(8,128)(2,1)} %a_hbm.1, bf16[3072,512]{1,0:T(8,128)(2,1)} %s_hbm.1, s32[1,3072]{1,0:T(1,128)} %bitcast.4, s32[1,3072]{1,0:T(1,128)} %bitcast.5, s32[1,512]{1,0:T(1,128)} %bitcast.6, f32[1,512]{1,0:T(1,128)} %bitcast.7), custom_call_target="tpu_custom_call" | custom-call | tf_op jit(solution)/shard_map/project/pallas_call | solution.py:473
  91.1 0.9 hand_over.1

commit v5 on v4

--- a/solution.py
+++ b/solution.py
@@ -15,28 +15,28 @@
 TILE = 512
 PARTS = 3
 SUM_MODE = "BABB"
-SPREAD_MODE = "BBBB"
+SPREAD_MODE = "BBAB"
 PANEL_MODE = "BBABBBBBBBBB"
 ORDER = (
-    ("A", 0), ("A", 1), ("Q", 0, 0), ("Q", 1, 0), ("A", 2), ("L", 0), ("Q", 0, 1), ("Q", 0, 2),
-    ("A", 3), ("Q", 0, 3), ("R2", 0), ("Q", 1, 1), ("Q", 1, 2), ("L", 2), ("Q", 1, 3), ("R2", 1),
-    ("C",), ("B", 0), ("R5", 0), ("R3", 0), ("B", 1), ("Q", 2, 0), ("B", 2), ("Q", 2, 1),
-    ("L", 3), ("Q", 2, 2), ("R3", 1), ("L", 1), ("R4", 0), ("B", 3), ("R4", 1), ("Q", 2, 3),
-    ("R2", 2), ("G2", 0), ("G5", 0), ("Q", 3, 0), ("G2", 1), ("G5", 1), ("R5", 2), ("G3", 0),
-    ("R3", 2), ("Q", 3, 1), ("Q", 3, 2), ("G4", 0), ("Q", 3, 3), ("V", 0), ("R2", 3), ("G3", 1),
-    ("W", 0), ("F0", 0, 1, 0), ("F1", 0, 1), ("F0", 0, 2, 0), ("R4", 2), ("F1", 0, 2), ("G4", 1), ("V", 1),
-    ("R3", 3), ("F0", 0, 0, 0), ("F1", 0, 0), ("R5", 3), ("W", 1), ("F0", 1, 1, 0), ("F1", 1, 1), ("G2", 2),
-    ("F0", 1, 2, 0), ("F0", 1, 0, 0), ("F2", 0, 2), ("F2", 0, 1), ("F1", 1, 0), ("R4", 3), ("F1", 1, 2), ("G5", 2),
-    ("F2", 1, 1), ("G3", 2), ("F2", 0, 0), ("F2", 1, 0), ("F3", 1, 0), ("F3", 0, 2), ("F5", 0, 1), ("G2", 3),
-    ("F5", 1, 1), ("F2", 1, 2), ("G5", 3), ("F5", 0, 0), ("F5", 1, 0), ("G4", 2), ("G3", 3), ("V", 2),
-    ("W", 2), ("F0", 2, 0, 0), ("F1", 2, 0), ("F0", 2, 2, 0), ("F5", 1, 2), ("F0", 2, 1, 0), ("F1", 2, 2), ("F1", 2, 1),
-    ("G4", 3), ("V", 3), ("F3", 1, 1), ("W", 3), ("F0", 3, 2, 0), ("F1", 3, 2), ("F0", 3, 0, 0), ("F3", 0, 1),
-    ("F2", 2, 2), ("F0", 3, 1, 0), ("F2", 2, 0), ("S0",), ("F1", 3, 1), ("F2", 2, 1), ("S", 0), ("F1", 3, 0),
-    ("F3", 2, 2), ("S", 1), ("F3", 1, 2), ("S", 2), ("F3", 2, 1), ("F3", 2, 0), ("F4", 0, 2), ("F5", 2, 0),
-    ("S", 3), ("F2", 3, 2), ("F4", 0, 1), ("F2", 3, 1), ("F4", 1, 1), ("S1",), ("F5", 2, 1), ("F2", 3, 0),
-    ("F3", 3, 1), ("F3", 3, 0), ("S2",), ("F5", 2, 2), ("F3", 3, 2), ("F5", 3, 1), ("F4", 1, 0), ("F5", 3, 2),
-    ("F5", 3, 0), ("S3",), ("F4", 2, 1), ("F3", 0, 0), ("S4",), ("F4", 1, 2), ("F4", 2, 2), ("F4", 2, 0),
-    ("F4", 0, 0), ("F4", 3, 1), ("F4", 3, 2), ("F4", 3, 0),
+    ("A", 0), ("A", 1), ("Q", 0, 0), ("Q", 1, 0), ("A", 2), ("L", 1), ("Q", 0, 1), ("Q", 0, 2),
+    ("A", 3), ("Q", 0, 3), ("R2", 0), ("Q", 1, 1), ("Q", 1, 2), ("C",), ("B", 0), ("R3", 0),
+    ("Q", 1, 3), ("R5", 0), ("R2", 1), ("L", 0), ("Q", 2, 0), ("B", 1), ("B", 2), ("R4", 0),
+    ("B", 3), ("Q", 2, 1), ("Q", 2, 2), ("R3", 1), ("Q", 2, 3), ("Q", 3, 0), ("R2", 2), ("L", 2),
+    ("L", 3), ("G2", 0), ("R4", 1), ("G5", 0), ("G3", 0), ("G2", 1), ("R5", 2), ("G5", 1),
+    ("Q", 3, 1), ("R3", 2), ("G4", 0), ("V", 0), ("W", 0), ("G3", 1), ("F0", 0, 2, 0), ("F1", 0, 2),
+    ("Q", 3, 2), ("Q", 3, 3), ("R2", 3), ("F0", 0, 1, 0), ("F1", 0, 1), ("F0", 0, 0, 0), ("R4", 2), ("F1", 0, 0),
+    ("G4", 1), ("F2", 0, 2), ("V", 1), ("W", 1), ("R3", 3), ("F0", 1, 1, 0), ("R5", 3), ("F2", 0, 1),
+    ("F0", 1, 2, 0), ("F1", 1, 1), ("F0", 1, 0, 0), ("G5", 2), ("F1", 1, 2), ("F1", 1, 0), ("F2", 0, 0), ("R4", 3),
+    ("F2", 1, 1), ("F3", 0, 1), ("G2", 2), ("G3", 2), ("F5", 0, 1), ("F2", 1, 2), ("F2", 1, 0), ("F5", 0, 0),
+    ("G2", 3), ("F5", 1, 1), ("F3", 1, 0), ("G5", 3), ("G4", 2), ("F3", 1, 1), ("V", 2), ("F5", 1, 2),
+    ("W", 2), ("F5", 1, 0), ("G3", 3), ("F0", 2, 1, 0), ("F0", 2, 0, 0), ("F1", 2, 0), ("F1", 2, 1), ("F0", 2, 2, 0),
+    ("F1", 2, 2), ("G4", 3), ("F3", 1, 2), ("V", 3), ("W", 3), ("F0", 3, 0, 0), ("F2", 2, 0), ("F1", 3, 0),
+    ("F0", 3, 2, 0), ("F1", 3, 2), ("F0", 3, 1, 0), ("F1", 3, 1), ("F3", 2, 0), ("S0",), ("F4", 1, 0), ("F5", 2, 0),
+    ("F2", 3, 0), ("F3", 3, 0), ("F2", 2, 2), ("F2", 2, 1), ("F2", 3, 2), ("S", 0), ("S", 1), ("F3", 2, 2),
+    ("F2", 3, 1), ("S", 2), ("F3", 0, 0), ("F3", 2, 1), ("F3", 3, 1), ("S", 3), ("S1",), ("F5", 2, 1),
+    ("F5", 2, 2), ("S2",), ("F5", 3, 0), ("F5", 3, 1), ("F3", 0, 2), ("F4", 0, 0), ("F3", 3, 2), ("F5", 3, 2),
+    ("S3",), ("F4", 2, 2), ("F4", 1, 2), ("F4", 2, 1), ("F4", 2, 0), ("F4", 3, 0), ("F4", 0, 1), ("F4", 1, 1),
+    ("F4", 3, 1), ("S4",), ("F4", 0, 2), ("F4", 3, 2),
 )
 
 

time: 92.3 us -> 92.5 us (level)
  no operation moved by 1% of the time
where the time goes in v5:
time: 92.5 us; the launch traced here: 92.3 us
  Pallas kernels  91.5 us (99%)
    pallas_call x1, Pallas kernels, body(): pl.pallas_call(kernel, name='project', out_shape=(pltpu.VMEM((nb // 8, de...  90.6 us

profile of v5, /device:TPU:0, one launch (start us, length us, event | category | flops | bytes accessed | tf_op | source)
XLA Modules:
  0.0 92.3 jit_solution(2732772023176846446)
XLA Ops:
  0.6 90.6 %project.1 = (f32[64,3072]{1,0:T(8,128)S(1)}, f32[32,64]{1,0:T(8,128)S(1)}) custom-call(bf16[3072,3072]{1,0:T(8,128)(2,1)} %a_hbm.1, bf16[3072,512]{1,0:T(8,128)(2,1)} %s_hbm.1, s32[1,3072]{1,0:T(1,128)} %bitcast.4, s32[1,3072]{1,0:T(1,128)} %bitcast.5, s32[1,512]{1,0:T(1,128)} %bitcast.6, f32[1,512]{1,0:T(1,128)} %bitcast.7), custom_call_target="tpu_custom_call" | custom-call | tf_op jit(solution)/shard_map/project/pallas_call | solution.py:473
  91.2 0.9 hand_over.1

commit v6 on v5

--- a/solution.py
+++ b/solution.py
@@ -445,10 +445,12 @@
 def hand_over(*arrays):
     def kernel(*refs):
         sources, targets, sem = refs[: len(arrays)], refs[len(arrays) : 2 * len(arrays)], refs[-1]
-        copies = [
-            pltpu.make_async_copy(source, target, sem.at[n])
-            for n, (source, target) in enumerate(zip(sources, targets))
-        ]
+        copies = []
+        for n, (source, target) in enumerate(zip(sources, targets)):
+            rows = source.shape[0] // 4
+            for i in range(4):
+                at = pl.ds(i * rows, rows)
+                copies.append(pltpu.make_async_copy(source.at[at], target.at[at], sem.at[n, i]))
         for copy in copies:
             copy.start()
         for copy in copies:
@@ -460,7 +462,7 @@
         out_shape=tuple(jax.ShapeDtypeStruct(v.shape, v.dtype) for v in arrays),
         in_specs=[pl.BlockSpec(memory_space=pltpu.VMEM)] * len(arrays),
         out_specs=tuple(pl.BlockSpec(memory_space=pl.ANY) for _ in arrays),
-        scratch_shapes=[pltpu.SemaphoreType.DMA((len(arrays),))],
+        scratch_shapes=[pltpu.SemaphoreType.DMA((len(arrays), 4))],
         compiler_params=pltpu.CompilerParams(vmem_limit_bytes=1 << 20),
     )(*arrays)
 

time: 92.5 us -> 92.5 us (level)
  no operation moved by 1% of the time
where the time goes in v6:
time: 92.5 us; the launch traced here: 92.4 us
  Pallas kernels  91.5 us (99%)
    pallas_call x1, Pallas kernels, body(): pl.pallas_call(kernel, name='project', out_shape=(pltpu.VMEM((nb // 8, de...  90.6 us

profile of v6, /device:TPU:0, one launch (start us, length us, event | category | flops | bytes accessed | tf_op | source)
XLA Modules:
  0.0 92.4 jit_solution(7978708509116776574)
XLA Ops:
  0.6 90.6 %project.1 = (f32[64,3072]{1,0:T(8,128)S(1)}, f32[32,64]{1,0:T(8,128)S(1)}) custom-call(bf16[3072,3072]{1,0:T(8,128)(2,1)} %a_hbm.1, bf16[3072,512]{1,0:T(8,128)(2,1)} %s_hbm.1, s32[1,3072]{1,0:T(1,128)} %bitcast.4, s32[1,3072]{1,0:T(1,128)} %bitcast.5, s32[1,512]{1,0:T(1,128)} %bitcast.6, f32[1,512]{1,0:T(1,128)} %bitcast.7), custom_call_target="tpu_custom_call" | custom-call | tf_op jit(solution)/shard_map/project/pallas_call | solution.py:475
  91.2 1.0 %hand_over.1 = (f32[64,3072]{1,0:T(8,128)}, f32[32,64]{1,0:T(8,128)}) custom-call(f32[64,3072]{1,0:T(8,128)S(1)} %get-tuple-element.4.refs_0_, f32[32,64]{1,0:T(8,128)S(1)} %get-tuple-element.5.refs_1_), custom_call_target="tpu_custom_call" | custom-call | tf_op jit(solution)/shard_map/hand_over/pallas_call | solution.py:459
